TPU v7x, 32 devices: a whole 2x2x4 slice. The times are simulated.
32 devices in a mesh: slab: 2 (over x), row: 8 (over z, y), col: 2 (over core).
Axes of the slice: x: 2, y: 2, z: 4, core: 2. Of those that a mesh axis runs over, the one named last changes fastest.
Arguments:
- points: bfloat16 [9, 32, 131072], P(None, None, ('slab', 'row', 'col')), parts along dimension 2, may hold values from -6 to 6
- pillar_cell: int32 [131072], P(('slab', 'row', 'col')), parts along dimension 0, may hold values from 0 to 65535, as said below
- point_count: int32 [131072], P(('slab', 'row', 'col')), parts along dimension 0, may hold values from 1 to 32
- tile_count: int32 [512], P(('slab', 'row', 'col')), parts along dimension 0, may hold values from 0 to 256, as said below
- point_embed: bfloat16 [64, 9], replicated, may hold values from -3 to 3
- point_mix: bfloat16 [64, 64], replicated, may hold values from -1 to 1
- first_conv: bfloat16 [3, 3, 64, 64], replicated, may hold values from -0.375 to 0.375
- second_conv: bfloat16 [3, 3, 64, 64], replicated, may hold values from -0.375 to 0.375
- third_conv: bfloat16 [3, 3, 128, 64], replicated, may hold values from -0.375 to 0.375
- fourth_conv: bfloat16 [3, 3, 128, 128], replicated, may hold values from -0.25 to 0.25
- fifth_conv: bfloat16 [3, 3, 256, 128], replicated, may hold values from -0.25 to 0.25
- sixth_conv: bfloat16 [3, 3, 256, 256], replicated, may hold values from -0.1875 to 0.1875
- near_lift: bfloat16 [1, 1, 128, 64], replicated, may hold values from -1 to 1
- mid_lift: bfloat16 [2, 2, 128, 128], replicated, may hold values from -0.75 to 0.75
- far_lift: bfloat16 [4, 4, 128, 256], replicated, may hold values from -0.5 to 0.5
- biases: float32 [1408], replicated, may hold values from -1.5 to 1.5
Outputs:
- joined: bfloat16 [384, 256, 512], P(None, ('slab', 'row'), 'col'), parts along dimension 1
There are 2 independent parts, one for each index of `slab`. A program takes and returns all parts, laid end to end along the dimension named above; an argument that names none is the same for every part. Nothing has to cross between parts.
Inputs may be any that keep to these rules, and one draw needn't show every extreme that they name: `tile_count`: entry s * 16 + t counts the live slots that device s (row-major over row and col) holds for tile t (row-major over row and col); they are the first of that tile's group of 256 slots. In every draw some tile gets exactly 256 live slots from every device. `pillar_cell`: slot s holds cell r * 512 + c; every slot in a device's group for tile t lies in tile t, whose rows and columns are those of device t; a cell may appear in several slots, on one device or several. `point_count`: the valid points of a slot are its first ones.
All inputs are finite; a program needn't handle non-finite values.
Results may differ from a plain program's by a relative error of at most 0.0081.
Values may be sent and summed in bfloat16 or wider, within the bound.
A program may use at most 64 MiB of HBM per device.

v0:
```python
import jax
import jax.numpy as jnp
from jax import lax
from jax.sharding import PartitionSpec as P

ROWS_DEV = 16
COLS_DEV = 256


def with_halo(block, sides, width):
    for axis, dim in sides:
        count = lax.axis_size(axis)
        forward = [(i, i + 1) for i in range(count - 1)]
        backward = [(target, source) for source, target in forward]
        low = lax.ppermute(
            lax.slice_in_dim(block, block.shape[dim] - width, None, axis=dim), axis, forward
        )
        high = lax.ppermute(lax.slice_in_dim(block, 0, width, axis=dim), axis, backward)
        block = jnp.concatenate([low, block, high], axis=dim)
    return block


def encode_block(point_block, count_row, point_embed, point_mix, b_embed, b_mix):
    feat_in, point_num, slot_num = point_block.shape
    flat_rows = point_block.reshape(feat_in, point_num * slot_num)
    hidden = jnp.dot(point_embed, flat_rows, preferred_element_type=jnp.float32) + b_embed[:, None]
    hidden = jax.nn.relu(hidden).astype(jnp.bfloat16)
    second = jnp.dot(point_mix, hidden, preferred_element_type=jnp.float32) + b_mix[:, None]
    second = jax.nn.relu(second).reshape(-1, point_num, slot_num)
    valid_mask = lax.broadcasted_iota(jnp.int32, (point_num, slot_num), 0) < count_row[None, :]
    return jnp.max(jnp.where(valid_mask[None], second, 0.0), axis=1).astype(jnp.bfloat16)


def conv_padded(padded, kernel, bias_vec, stride):
    rows_out = (padded.shape[1] - 2) // stride
    cols_out = (padded.shape[2] - 2) // stride
    summed = jnp.zeros((kernel.shape[2], rows_out, cols_out), jnp.float32)
    for tap_row in range(3):
        for tap_col in range(3):
            window = padded[
                :,
                tap_row : tap_row + stride * rows_out : stride,
                tap_col : tap_col + stride * cols_out : stride,
            ]
            summed = summed + jnp.einsum(
                "oc,chw->ohw", kernel[tap_row, tap_col], window, preferred_element_type=jnp.float32
            )
    return jax.nn.relu(summed + bias_vec[:, None, None]).astype(jnp.bfloat16)


def conv_tiles(inputs, kernel, bias_vec, stride):
    padded = with_halo(inputs, (("row", 1), ("col", 2)), 1)
    return conv_padded(padded, kernel, bias_vec, stride)


def lift_layer(inputs, kernel, bias_vec):
    factor = kernel.shape[0]
    product = jnp.einsum("abop,pij->oiajb", kernel, inputs, preferred_element_type=jnp.float32)
    product = product.reshape(kernel.shape[2], inputs.shape[1] * factor, inputs.shape[2] * factor)
    return jax.nn.relu(product + bias_vec[:, None, None]).astype(jnp.bfloat16)


def on_device(
    points,
    pillar_cell,
    point_count,
    tile_count,
    point_embed,
    point_mix,
    first_conv,
    second_conv,
    third_conv,
    fourth_conv,
    fifth_conv,
    sixth_conv,
    near_lift,
    mid_lift,
    far_lift,
    biases,
):
    extents = [
        point_embed.shape[0],
        point_mix.shape[0],
        first_conv.shape[2],
        second_conv.shape[2],
        third_conv.shape[2],
        fourth_conv.shape[2],
        fifth_conv.shape[2],
        sixth_conv.shape[2],
        near_lift.shape[2],
        mid_lift.shape[2],
        far_lift.shape[2],
    ]
    pieces = []
    offset = 0
    for extent in extents:
        pieces.append(biases[offset : offset + extent])
        offset += extent
    feat_in, point_num, slot_total = points.shape
    tile_num = tile_count.shape[0]
    capacity = slot_total // tile_num
    ncols_all = COLS_DEV * lax.axis_size("col")
    live_slot = lax.broadcasted_iota(jnp.int32, (tile_num, capacity), 1) < tile_count[:, None]
    live_points = jnp.where(live_slot, point_count.reshape(tile_num, capacity), 0)
    row_global = pillar_cell // ncols_all
    local_cell = row_global % ROWS_DEV * COLS_DEV + pillar_cell % ncols_all % COLS_DEV
    local_cell = local_cell.reshape(tile_num, capacity)
    grouped = points.reshape(feat_in, point_num, tile_num, capacity)

    def encode_one(group_id):
        point_block = lax.dynamic_index_in_dim(grouped, group_id, 2, keepdims=False)
        count_row = lax.dynamic_index_in_dim(live_points, group_id, 0, keepdims=False)
        return encode_block(point_block, count_row, point_embed, point_mix, pieces[0], pieces[1])

    encoded = lax.map(encode_one, jnp.arange(grouped.shape[2], dtype=jnp.int32))
    vectors, cell_ids = (
        lax.all_to_all(encoded, ("row", "col"), split_axis=0, concat_axis=0, tiled=True),
        lax.all_to_all(
            local_cell.reshape(tile_num, 1, capacity),
            ("row", "col"),
            split_axis=0,
            concat_axis=0,
            tiled=True,
        ),
    )
    feature_rows = jnp.moveaxis(vectors, 1, 0).reshape(vectors.shape[1], -1)
    bev = jnp.zeros((feature_rows.shape[0], ROWS_DEV * COLS_DEV), jnp.bfloat16)
    bev = bev.at[:, cell_ids.reshape(-1)].max(feature_rows).reshape(-1, ROWS_DEV, COLS_DEV)
    level_one = conv_tiles(conv_tiles(bev, first_conv, pieces[2], 1), second_conv, pieces[3], 1)
    level_two = conv_tiles(
        conv_tiles(level_one, third_conv, pieces[4], 2), fourth_conv, pieces[5], 1
    )
    level_three = conv_tiles(
        conv_tiles(level_two, fifth_conv, pieces[6], 2), sixth_conv, pieces[7], 1
    )
    near = lift_layer(level_one, near_lift, pieces[8])
    middle = lift_layer(level_two, mid_lift, pieces[9])
    distant = lift_layer(level_three, far_lift, pieces[10])
    return jnp.concatenate([near, middle, distant], axis=0)


def solution(mesh):
    return jax.shard_map(
        on_device,
        mesh=mesh,
        in_specs=(
            P(None, None, ("slab", "row", "col")),
            P(("slab", "row", "col")),
            P(("slab", "row", "col")),
            P(("slab", "row", "col")),
            P(),
            P(),
            P(),
            P(),
            P(),
            P(),
            P(),
            P(),
            P(),
            P(),
            P(),
            P(),
        ),
        out_specs=P(None, ("slab", "row"), "col"),
        check_vma=False,
    )
```

profile of v0, /device:TPU:9, one launch (start us, length us, event | category | flops | bytes accessed | tf_op | source)
XLA Modules:
  0.0 329.4 jit_solution(8467874083410575611)
XLA Ops:
  1.4 6.6 %all-to-all-start = ((s32[16,1,256]{2,1,0:T(1,128)}), s32[16,1,256]{2,1,0:T(1,128)S(1)}, u32[]{:S(2)}, u32[]{:S(2)}) async-start(s32[16,1,256]{2,1,0:T(1,128)} %bitcast.4), calls=%async_computation | async-start | bytes 32768 | tf_op jit(solution)/shard_map/all_to_all | solution.py:118
  9.0 3.4 %copy.63 = bf16[9,4,16,8,256]{4,3,1,0,2:T(8,128)(2,1)} copy(bf16[9,4,16,8,256]{4,3,2,1,0:T(8,128)(2,1)} %bitcast.409) | data formatting | bytes 4718592 | tf_op jit(solution)/shard_map/reshape | solution.py:108
  12.5 96.6 %while.10 = (s32[]{:T(128)}, bf16[16,64,256]{2,1,0:T(8,128)(2,1)}, s32[16]{0:T(128)S(1)}, s32[16,256]{1,0:T(8,128)S(1)}, bf16[9,32,16,256]{3,1,0,2:T(8,128)(2,1)...) while((s32[]{:T(128)}, bf16[16,64,256]{2,1,0:T(8,128)(2,1)}, ...), condition=%wide.region_2.3_spmd, body=%wide.region_0.2_spmd.sunk | while | flops 80732160 | bytes 5698869 | solution.py:115
  109.7 6.0 %all-to-all-start.1 = ((bf16[16,64,256]{2,1,0:T(8,128)(2,1)}), bf16[16,64,256]{2,1,0:T(8,128)(2,1)S(1)}, u32[]{:S(2)}, u32[]{:S(2)}) async-start(bf16[16,64,256]{2,1,0:T(8,128)(2,1)} %get-tuple-element.52), calls=%async_computation.1 | async-start | bytes 1048576 | tf_op jit(solution)/shard_map/all_to_all | solution.py:117
  115.7 14.1 %all-to-all-done.1 = bf16[16,64,256]{2,1,0:T(8,128)(2,1)S(1)} async-done(((bf16[16,64,256]{2,1,0:T(8,128)(2,1)}), bf16[16,64,256]{2,1,0:T(8,128)(2,1)S(1)}, u32[]{:S(2)}, u32[]{:S(2)}) %all-to-all-start.1) | async-done | bytes 524320 | tf_op jit(solution)/shard_map/all_to_all | solution.py:117
  131.2 23.2 %scatter_custom_fusion = bf16[64,4096]{0,1:T(8,128)(2,1)S(1)} fusion(s32[4096]{0:T(1024)S(1)} %bitcast.414, bf16[4096,64]{1,0:T(8,128)(2,1)} %copy.36, bf16[]{:T(256)} %constant.82.clone.1), kind=kCustom, calls=%fused_computation.136 | custom fusion | flops 262144 | bytes 524800 | tf_op jit(solution)/shard_map/scatter-max | solution.py:128
  157.3 3.6 %collective-permute-start.1 = (bf16[64,1,256]{2,0,1:T(8,128)(2,1)S(1)}, bf16[64,1,256]{2,0,1:T(8,128)(2,1)S(1)}, u32[]{:S(2)}, u32[]{:S(2)}) collective-permute-start(bf16[64,1,256]{2,0,1:T(8,128)(2,1)S(1)} %get-tuple-element.95), channel_id=1, source_target_pairs={{2,0},{4,2},{6,4},{8,6},{10,8},{12,10},{14,12},{3,1},{5,3},{7,5},{... | collective-permute-start | bytes 98312 | tf_op jit(solution)/shard_map/ppermute | solution.py:18
  163.5 3.5 %collective-permute-start.3 = (bf16[64,18,1]{2,0,1:T(8,128)(2,1)S(1)}, bf16[64,18,1]{2,0,1:T(8,128)(2,1)S(1)}, u32[]{:S(2)}, u32[]{:S(2)}) collective-permute-start(bf16[64,18,1]{2,0,1:T(8,128)(2,1)S(1)} %get-tuple-element.89), channel_id=1, source_target_pairs={{1,0},{3,2},{5,4},{7,6},{9,8},{11,10},{13,12},{15,14},{17,16},{19,... | collective-permute-start | bytes 6920 | tf_op jit(solution)/shard_map/ppermute | solution.py:18
  171.1 4.5 %collective-permute-start.4 = (bf16[64,1,256]{2,0,1:T(8,128)(2,1)S(1)}, bf16[64,1,256]{2,0,1:T(8,128)(2,1)S(1)}, u32[]{:S(2)}, u32[]{:S(2)}) collective-permute-start(bf16[64,1,256]{2,0,1:T(8,128)(2,1)S(1)} %get-tuple-element.92), channel_id=1, source_target_pairs={{0,2},{2,4},{4,6},{6,8},{8,10},{10,12},{12,14},{1,3},{3,5},{5,7},{... | collective-permute-start | bytes 98312 | tf_op jit(solution)/shard_map/ppermute | solution.py:15
  181.8 3.9 %collective-permute-start.7 = (bf16[64,18,1]{2,0,1:T(8,128)(2,1)S(1)}, bf16[64,18,1]{2,0,1:T(8,128)(2,1)S(1)}, u32[]{:S(2)}, u32[]{:S(2)}) collective-permute-start(bf16[64,18,1]{2,0,1:T(8,128)(2,1)S(1)} %get-tuple-element.85), channel_id=1, source_target_pairs={{1,0},{3,2},{5,4},{7,6},{9,8},{11,10},{13,12},{15,14},{17,16},{19,... | collective-permute-start | bytes 6920 | tf_op jit(solution)/shard_map/ppermute | solution.py:18
  189.7 5.0 %slice.508 = bf16[64,8,128]{2,0,1:T(8,128)(2,1)S(1)} slice(bf16[64,16,256]{2,0,1:T(8,128)(2,1)S(1)} %fusion.27), slice={[0:64:1], [0:16:2], [0:256:2]} | slice | bytes 262144 | tf_op jit(solution)/shard_map/slice | solution.py:40
  194.7 2.6 collective-permute-start.8
  197.3 3.6 %collective-permute-start.9 = (bf16[64,1,256]{2,0,1:T(8,128)(2,1)S(1)}, bf16[64,1,256]{2,0,1:T(8,128)(2,1)S(1)}, u32[]{:S(2)}, u32[]{:S(2)}) collective-permute-start(bf16[64,1,256]{2,0,1:T(8,128)(2,1)S(1)} %get-tuple-element.91), channel_id=1, source_target_pairs={{2,0},{4,2},{6,4},{8,6},{10,8},{12,10},{14,12},{3,1},{5,3},{7,5},{... | collective-permute-start | bytes 98312 | tf_op jit(solution)/shard_map/ppermute | solution.py:18
  204.2 5.0 %slice.502 = bf16[64,8,128]{2,0,1:T(8,128)(2,1)S(1)} slice(bf16[64,18,256]{2,0,1:T(8,128)(2,1)S(1)} %pad_maximum_fusion.6), slice={[0:64:1], [0:16:2], [0:256:2]} | slice | bytes 262144 | tf_op jit(solution)/shard_map/slice | solution.py:40
  209.3 5.0 %slice.514 = bf16[64,8,128]{2,0,1:T(8,128)(2,1)S(1)} slice(bf16[64,18,256]{2,0,1:T(8,128)(2,1)S(1)} %pad_maximum_fusion.6), slice={[0:64:1], [2:18:2], [0:256:2]} | slice | bytes 262144 | tf_op jit(solution)/shard_map/slice | solution.py:40
  215.6 3.1 collective-permute-start.11
  222.8 5.6 %slice.506 = bf16[64,8,128]{2,0,1:T(8,128)(2,1)} slice(bf16[64,18,258]{2,0,1:T(8,128)(2,1)S(1)} %pad_maximum_fusion.3), slice={[0:64:1], [1:17:2], [0:256:2]} | slice | bytes 262144 | tf_op jit(solution)/shard_map/slice | solution.py:40
  228.4 5.7 %slice.504 = bf16[64,8,128]{2,0,1:T(8,128)(2,1)} slice(bf16[64,18,258]{2,0,1:T(8,128)(2,1)S(1)} %pad_maximum_fusion.3), slice={[0:64:1], [0:16:2], [2:258:2]} | slice | bytes 262144 | tf_op jit(solution)/shard_map/slice | solution.py:40
  234.1 5.6 %slice.500 = bf16[64,8,128]{2,0,1:T(8,128)(2,1)} slice(bf16[64,18,258]{2,0,1:T(8,128)(2,1)S(1)} %pad_maximum_fusion.3), slice={[0:64:1], [0:16:2], [0:256:2]} | slice | bytes 262144 | tf_op jit(solution)/shard_map/slice | solution.py:40
  239.7 5.7 %slice.516 = bf16[64,8,128]{2,0,1:T(8,128)(2,1)} slice(bf16[64,18,258]{2,0,1:T(8,128)(2,1)S(1)} %pad_maximum_fusion.3), slice={[0:64:1], [2:18:2], [2:258:2]} | slice | bytes 262144 | tf_op jit(solution)/shard_map/slice | solution.py:40
  245.4 5.6 %slice.512 = bf16[64,8,128]{2,0,1:T(8,128)(2,1)} slice(bf16[64,18,258]{2,0,1:T(8,128)(2,1)S(1)} %pad_maximum_fusion.3), slice={[0:64:1], [2:18:2], [0:256:2]} | slice | bytes 262144 | tf_op jit(solution)/shard_map/slice | solution.py:40
  251.0 5.7 %slice.510 = bf16[64,8,128]{2,0,1:T(8,128)(2,1)} slice(bf16[64,18,258]{2,0,1:T(8,128)(2,1)S(1)} %pad_maximum_fusion.3), slice={[0:64:1], [1:17:2], [2:258:2]} | slice | bytes 262144 | tf_op jit(solution)/shard_map/slice | solution.py:40
  265.4 4.3 %collective-permute-start.13 = (bf16[128,1,128]{0,2,1:T(8,128)(2,1)S(1)}, bf16[128,1,128]{0,2,1:T(8,128)(2,1)S(1)}, u32[]{:S(2)}, u32[]{:S(2)}) collective-permute-start(bf16[128,1,128]{0,2,1:T(8,128)(2,1)S(1)} %get-tuple-element.105), channel_id=1, source_target_pairs={{2,0},{4,2},{6,4},{8,6},{10,8},{12,10},{14,12},{3,1},{5,3},{7,5},{... | collective-permute-start | bytes 98312 | tf_op jit(solution)/shard_map/ppermute | solution.py:18
  272.0 3.2 collective-permute-start.15
  277.8 3.3 %collective-permute-start.16 = (bf16[128,1,128]{0,2,1:T(8,128)(2,1)S(1)}, bf16[128,1,128]{0,2,1:T(8,128)(2,1)S(1)}, u32[]{:S(2)}, u32[]{:S(2)}) collective-permute-start(bf16[128,1,128]{0,2,1:T(8,128)(2,1)S(1)} %get-tuple-element.102), channel_id=1, source_target_pairs={{0,2},{2,4},{4,6},{6,8},{8,10},{10,12},{12,14},{1,3},{3,5},{5,7},{... | collective-permute-start | bytes 98312 | tf_op jit(solution)/shard_map/ppermute | solution.py:15
  281.1 3.6 %collective-permute-start.17 = (bf16[128,1,128]{0,2,1:T(8,128)(2,1)S(1)}, bf16[128,1,128]{0,2,1:T(8,128)(2,1)S(1)}, u32[]{:S(2)}, u32[]{:S(2)}) collective-permute-start(bf16[128,1,128]{0,2,1:T(8,128)(2,1)S(1)} %get-tuple-element.103), channel_id=1, source_target_pairs={{2,0},{4,2},{6,4},{8,6},{10,8},{12,10},{14,12},{3,1},{5,3},{7,5},{... | collective-permute-start | bytes 98312 | tf_op jit(solution)/shard_map/ppermute | solution.py:18
  292.1 3.0 collective-permute-start.19
  301.6 4.3 %collective-permute-start.21 = (bf16[256,1,64]{0,2,1:T(8,128)(2,1)S(1)}, bf16[256,1,64]{0,2,1:T(8,128)(2,1)S(1)}, u32[]{:S(2)}, u32[]{:S(2)}) collective-permute-start(bf16[256,1,64]{0,2,1:T(8,128)(2,1)S(1)} %get-tuple-element.111), channel_id=1, source_target_pairs={{2,0},{4,2},{6,4},{8,6},{10,8},{12,10},{14,12},{3,1},{5,3},{7,5},{... | collective-permute-start | bytes 98312 | tf_op jit(solution)/shard_map/ppermute | solution.py:18
  308.2 3.0 collective-permute-start.23
  317.6 2.7 copy.46
  320.3 3.1 copy.47
  326.0 3.4 %copy.48 = bf16[384,16,256]{2,1,0:T(8,128)(2,1)} copy(bf16[384,16,256]{2,0,1:T(8,128)(2,1)S(1)} %pad_maximum_fusion) | data formatting | bytes 6291456 | tf_op jit(solution)/shard_map/concatenate | solution.py:139
  (346 shorter events, 133.3 us)
Async XLA Ops:
  0.0 315.8 %copy-start = (bf16[4,4,128,256]{3,2,1,0:T(8,128)(2,1)S(1)}, bf16[4,4,128,256]{3,2,1,0:T(8,128)(2,1)}, u32[]{:S(2)}) copy-start(bf16[4,4,128,256]{3,2,1,0:T(8,128)(2,1)} %param.32) | copy-start | bytes 3145732
  1.4 108.2 %all-to-all-start = ((s32[16,1,256]{2,1,0:T(1,128)}), s32[16,1,256]{2,1,0:T(1,128)S(1)}, u32[]{:S(2)}, u32[]{:S(2)}) async-start(s32[16,1,256]{2,1,0:T(1,128)} %bitcast.4), calls=%async_computation | async-start | bytes 32768 | tf_op jit(solution)/shard_map/all_to_all | solution.py:118
  12.5 96.6 %copy-start.17 = (f32[1408]{0:T(1024)S(1)}, f32[1408]{0:T(1024)}, u32[]{:S(2)}) copy-start(f32[1408]{0:T(1024)} %param.33) | copy-start | bytes 16900
  109.7 20.1 %all-to-all-start.1 = ((bf16[16,64,256]{2,1,0:T(8,128)(2,1)}), bf16[16,64,256]{2,1,0:T(8,128)(2,1)S(1)}, u32[]{:S(2)}, u32[]{:S(2)}) async-start(bf16[16,64,256]{2,1,0:T(8,128)(2,1)} %get-tuple-element.52), calls=%async_computation.1 | async-start | bytes 1048576 | tf_op jit(solution)/shard_map/all_to_all | solution.py:117
  131.2 29.7 %copy-start.11 = (bf16[3,3,64,64]{3,2,1,0:T(8,128)(2,1)S(1)}, bf16[3,3,64,64]{3,2,1,0:T(8,128)(2,1)}, u32[]{:S(2)}) copy-start(bf16[3,3,64,64]{3,2,1,0:T(8,128)(2,1)} %param.24) | copy-start | bytes 221188
  154.7 6.7 %collective-permute-start = (bf16[64,1,256]{2,0,1:T(8,128)(2,1)S(1)}, bf16[64,1,256]{2,0,1:T(8,128)(2,1)S(1)}, u32[]{:S(2)}, u32[]{:S(2)}) collective-permute-start(bf16[64,1,256]{2,0,1:T(8,128)(2,1)S(1)} %get-tuple-element.94), channel_id=1, source_target_pairs={{0,2},{2,4},{4,6},{6,8},{8,10},{10,12},{12,14},{1,3},{3,5},{5,7},{... | collective-permute-start | bytes 98312 | tf_op jit(solution)/shard_map/ppermute | solution.py:15
  157.3 4.7 %collective-permute-start.1 = (bf16[64,1,256]{2,0,1:T(8,128)(2,1)S(1)}, bf16[64,1,256]{2,0,1:T(8,128)(2,1)S(1)}, u32[]{:S(2)}, u32[]{:S(2)}) collective-permute-start(bf16[64,1,256]{2,0,1:T(8,128)(2,1)S(1)} %get-tuple-element.95), channel_id=1, source_target_pairs={{2,0},{4,2},{6,4},{8,6},{10,8},{12,10},{14,12},{3,1},{5,3},{7,5},{... | collective-permute-start | bytes 98312 | tf_op jit(solution)/shard_map/ppermute | solution.py:18
  162.2 5.4 %collective-permute-start.2 = (bf16[64,18,1]{2,0,1:T(8,128)(2,1)S(1)}, bf16[64,18,1]{2,0,1:T(8,128)(2,1)S(1)}, u32[]{:S(2)}, u32[]{:S(2)}) collective-permute-start(bf16[64,18,1]{2,0,1:T(8,128)(2,1)S(1)} %get-tuple-element.88), channel_id=1, source_target_pairs={{0,1},{2,3},{4,5},{6,7},{8,9},{10,11},{12,13},{14,15},{16,17},{18,... | collective-permute-start | bytes 6920 | tf_op jit(solution)/shard_map/ppermute | solution.py:15
  163.5 4.7 %collective-permute-start.3 = (bf16[64,18,1]{2,0,1:T(8,128)(2,1)S(1)}, bf16[64,18,1]{2,0,1:T(8,128)(2,1)S(1)}, u32[]{:S(2)}, u32[]{:S(2)}) collective-permute-start(bf16[64,18,1]{2,0,1:T(8,128)(2,1)S(1)} %get-tuple-element.89), channel_id=1, source_target_pairs={{1,0},{3,2},{5,4},{7,6},{9,8},{11,10},{13,12},{15,14},{17,16},{19,... | collective-permute-start | bytes 6920 | tf_op jit(solution)/shard_map/ppermute | solution.py:18
  171.1 6.8 %collective-permute-start.4 = (bf16[64,1,256]{2,0,1:T(8,128)(2,1)S(1)}, bf16[64,1,256]{2,0,1:T(8,128)(2,1)S(1)}, u32[]{:S(2)}, u32[]{:S(2)}) collective-permute-start(bf16[64,1,256]{2,0,1:T(8,128)(2,1)S(1)} %get-tuple-element.92), channel_id=1, source_target_pairs={{0,2},{2,4},{4,6},{6,8},{8,10},{10,12},{12,14},{1,3},{3,5},{5,7},{... | collective-permute-start | bytes 98312 | tf_op jit(solution)/shard_map/ppermute | solution.py:15
  175.6 4.7 %collective-permute-start.5 = (bf16[64,1,256]{2,0,1:T(8,128)(2,1)S(1)}, bf16[64,1,256]{2,0,1:T(8,128)(2,1)S(1)}, u32[]{:S(2)}, u32[]{:S(2)}) collective-permute-start(bf16[64,1,256]{2,0,1:T(8,128)(2,1)S(1)} %get-tuple-element.93), channel_id=1, source_target_pairs={{2,0},{4,2},{6,4},{8,6},{10,8},{12,10},{14,12},{3,1},{5,3},{7,5},{... | collective-permute-start | bytes 98312 | tf_op jit(solution)/shard_map/ppermute | solution.py:18
  180.5 5.8 %collective-permute-start.6 = (bf16[64,18,1]{2,0,1:T(8,128)(2,1)S(1)}, bf16[64,18,1]{2,0,1:T(8,128)(2,1)S(1)}, u32[]{:S(2)}, u32[]{:S(2)}) collective-permute-start(bf16[64,18,1]{2,0,1:T(8,128)(2,1)S(1)} %get-tuple-element.84), channel_id=1, source_target_pairs={{0,1},{2,3},{4,5},{6,7},{8,9},{10,11},{12,13},{14,15},{16,17},{18,... | collective-permute-start | bytes 6920 | tf_op jit(solution)/shard_map/ppermute | solution.py:15
  181.8 4.9 %collective-permute-start.7 = (bf16[64,18,1]{2,0,1:T(8,128)(2,1)S(1)}, bf16[64,18,1]{2,0,1:T(8,128)(2,1)S(1)}, u32[]{:S(2)}, u32[]{:S(2)}) collective-permute-start(bf16[64,18,1]{2,0,1:T(8,128)(2,1)S(1)} %get-tuple-element.85), channel_id=1, source_target_pairs={{1,0},{3,2},{5,4},{7,6},{9,8},{11,10},{13,12},{15,14},{17,16},{19,... | collective-permute-start | bytes 6920 | tf_op jit(solution)/shard_map/ppermute | solution.py:18
  189.0 11.9 %copy-start.22 = (bf16[1,1,128,64]{2,3,1,0:T(8,128)(2,1)S(1)}, bf16[1,1,128,64]{2,3,1,0:T(8,128)(2,1)}, u32[]{:S(2)}) copy-start(bf16[1,1,128,64]{2,3,1,0:T(8,128)(2,1)} %param.30) | copy-start | bytes 49156
  194.7 8.7 %collective-permute-start.8 = (bf16[64,1,256]{2,0,1:T(8,128)(2,1)S(1)}, bf16[64,1,256]{2,0,1:T(8,128)(2,1)S(1)}, u32[]{:S(2)}, u32[]{:S(2)}) collective-permute-start(bf16[64,1,256]{2,0,1:T(8,128)(2,1)S(1)} %get-tuple-element.90), channel_id=1, source_target_pairs={{0,2},{2,4},{4,6},{6,8},{8,10},{10,12},{12,14},{1,3},{3,5},{5,7},{... | collective-permute-start | bytes 98312 | tf_op jit(solution)/shard_map/ppermute | solution.py:15
  197.3 6.1 %collective-permute-start.9 = (bf16[64,1,256]{2,0,1:T(8,128)(2,1)S(1)}, bf16[64,1,256]{2,0,1:T(8,128)(2,1)S(1)}, u32[]{:S(2)}, u32[]{:S(2)}) collective-permute-start(bf16[64,1,256]{2,0,1:T(8,128)(2,1)S(1)} %get-tuple-element.91), channel_id=1, source_target_pairs={{2,0},{4,2},{6,4},{8,6},{10,8},{12,10},{14,12},{3,1},{5,3},{7,5},{... | collective-permute-start | bytes 98312 | tf_op jit(solution)/shard_map/ppermute | solution.py:18
  214.3 7.1 %collective-permute-start.10 = (bf16[64,18,1]{2,0,1:T(8,128)(2,1)S(1)}, bf16[64,18,1]{2,0,1:T(8,128)(2,1)S(1)}, u32[]{:S(2)}, u32[]{:S(2)}) collective-permute-start(bf16[64,18,1]{2,0,1:T(8,128)(2,1)S(1)} %get-tuple-element.80), channel_id=1, source_target_pairs={{0,1},{2,3},{4,5},{6,7},{8,9},{10,11},{12,13},{14,15},{16,17},{18,... | collective-permute-start | bytes 6920 | tf_op jit(solution)/shard_map/ppermute | solution.py:15
  215.6 5.8 %collective-permute-start.11 = (bf16[64,18,1]{2,0,1:T(8,128)(2,1)S(1)}, bf16[64,18,1]{2,0,1:T(8,128)(2,1)S(1)}, u32[]{:S(2)}, u32[]{:S(2)}) collective-permute-start(bf16[64,18,1]{2,0,1:T(8,128)(2,1)S(1)} %get-tuple-element.81), channel_id=1, source_target_pairs={{1,0},{3,2},{5,4},{7,6},{9,8},{11,10},{13,12},{15,14},{17,16},{19,... | collective-permute-start | bytes 6920 | tf_op jit(solution)/shard_map/ppermute | solution.py:18
  239.7 21.5 %copy-start.2 = (f32[8,128,128]{2,1,0:T(8,128)S(1)}, f32[8,128,128]{2,1,0:T(8,128)}, u32[]{:S(2)}) copy-start(f32[8,128,128]{2,1,0:T(8,128)} %fusion.222) | copy-start | bytes 1572868
  263.4 6.4 %collective-permute-start.12 = (bf16[128,1,128]{0,2,1:T(8,128)(2,1)S(1)}, bf16[128,1,128]{0,2,1:T(8,128)(2,1)S(1)}, u32[]{:S(2)}, u32[]{:S(2)}) collective-permute-start(bf16[128,1,128]{0,2,1:T(8,128)(2,1)S(1)} %get-tuple-element.104), channel_id=1, source_target_pairs={{0,2},{2,4},{4,6},{6,8},{8,10},{10,12},{12,14},{1,3},{3,5},{5,7},{... | collective-permute-start | bytes 98312 | tf_op jit(solution)/shard_map/ppermute | solution.py:15
  265.4 5.3 %collective-permute-start.13 = (bf16[128,1,128]{0,2,1:T(8,128)(2,1)S(1)}, bf16[128,1,128]{0,2,1:T(8,128)(2,1)S(1)}, u32[]{:S(2)}, u32[]{:S(2)}) collective-permute-start(bf16[128,1,128]{0,2,1:T(8,128)(2,1)S(1)} %get-tuple-element.105), channel_id=1, source_target_pairs={{2,0},{4,2},{6,4},{8,6},{10,8},{12,10},{14,12},{3,1},{5,3},{7,5},{... | collective-permute-start | bytes 98312 | tf_op jit(solution)/shard_map/ppermute | solution.py:18
  270.7 5.0 %collective-permute-start.14 = (bf16[128,10,1]{0,2,1:T(2,128)(2,1)S(1)}, bf16[128,10,1]{0,2,1:T(2,128)(2,1)S(1)}, u32[]{:S(2)}, u32[]{:S(2)}) collective-permute-start(bf16[128,10,1]{0,2,1:T(2,128)(2,1)S(1)} %get-tuple-element.100), channel_id=1, source_target_pairs={{0,1},{2,3},{4,5},{6,7},{8,9},{10,11},{12,13},{14,15},{16,17},{18,... | collective-permute-start | bytes 7688 | tf_op jit(solution)/shard_map/ppermute | solution.py:15
  272.0 3.8 %collective-permute-start.15 = (bf16[128,10,1]{0,2,1:T(2,128)(2,1)S(1)}, bf16[128,10,1]{0,2,1:T(2,128)(2,1)S(1)}, u32[]{:S(2)}, u32[]{:S(2)}) collective-permute-start(bf16[128,10,1]{0,2,1:T(2,128)(2,1)S(1)} %get-tuple-element.101), channel_id=1, source_target_pairs={{1,0},{3,2},{5,4},{7,6},{9,8},{11,10},{13,12},{15,14},{17,16},{19,... | collective-permute-start | bytes 7688 | tf_op jit(solution)/shard_map/ppermute | solution.py:18
  277.8 12.6 %collective-permute-start.16 = (bf16[128,1,128]{0,2,1:T(8,128)(2,1)S(1)}, bf16[128,1,128]{0,2,1:T(8,128)(2,1)S(1)}, u32[]{:S(2)}, u32[]{:S(2)}) collective-permute-start(bf16[128,1,128]{0,2,1:T(8,128)(2,1)S(1)} %get-tuple-element.102), channel_id=1, source_target_pairs={{0,2},{2,4},{4,6},{6,8},{8,10},{10,12},{12,14},{1,3},{3,5},{5,7},{... | collective-permute-start | bytes 98312 | tf_op jit(solution)/shard_map/ppermute | solution.py:15
  281.1 9.3 %collective-permute-start.17 = (bf16[128,1,128]{0,2,1:T(8,128)(2,1)S(1)}, bf16[128,1,128]{0,2,1:T(8,128)(2,1)S(1)}, u32[]{:S(2)}, u32[]{:S(2)}) collective-permute-start(bf16[128,1,128]{0,2,1:T(8,128)(2,1)S(1)} %get-tuple-element.103), channel_id=1, source_target_pairs={{2,0},{4,2},{6,4},{8,6},{10,8},{12,10},{14,12},{3,1},{5,3},{7,5},{... | collective-permute-start | bytes 98312 | tf_op jit(solution)/shard_map/ppermute | solution.py:18
  290.4 8.1 %copy-start.6 = (bf16[3,3,256,128]{3,2,1,0:T(8,128)(2,1)S(1)}, bf16[3,3,256,128]{3,2,1,0:T(8,128)(2,1)}, u32[]{:S(2)}) copy-start(bf16[3,3,256,128]{3,2,1,0:T(8,128)(2,1)} %param.28) | copy-start | bytes 1769476
  290.8 6.5 %collective-permute-start.18 = (bf16[128,10,1]{0,2,1:T(2,128)(2,1)S(1)}, bf16[128,10,1]{0,2,1:T(2,128)(2,1)S(1)}, u32[]{:S(2)}, u32[]{:S(2)}) collective-permute-start(bf16[128,10,1]{0,2,1:T(2,128)(2,1)S(1)} %get-tuple-element.96), channel_id=1, source_target_pairs={{0,1},{2,3},{4,5},{6,7},{8,9},{10,11},{12,13},{14,15},{16,17},{18,... | collective-permute-start | bytes 7688 | tf_op jit(solution)/shard_map/ppermute | solution.py:15
  292.1 5.2 %collective-permute-start.19 = (bf16[128,10,1]{0,2,1:T(2,128)(2,1)S(1)}, bf16[128,10,1]{0,2,1:T(2,128)(2,1)S(1)}, u32[]{:S(2)}, u32[]{:S(2)}) collective-permute-start(bf16[128,10,1]{0,2,1:T(2,128)(2,1)S(1)} %get-tuple-element.97), channel_id=1, source_target_pairs={{1,0},{3,2},{5,4},{7,6},{9,8},{11,10},{13,12},{15,14},{17,16},{19,... | collective-permute-start | bytes 7688 | tf_op jit(solution)/shard_map/ppermute | solution.py:18
  299.7 6.4 %collective-permute-start.20 = (bf16[256,1,64]{0,2,1:T(8,128)(2,1)S(1)}, bf16[256,1,64]{0,2,1:T(8,128)(2,1)S(1)}, u32[]{:S(2)}, u32[]{:S(2)}) collective-permute-start(bf16[256,1,64]{0,2,1:T(8,128)(2,1)S(1)} %get-tuple-element.110), channel_id=1, source_target_pairs={{0,2},{2,4},{4,6},{6,8},{8,10},{10,12},{12,14},{1,3},{3,5},{5,7},{... | collective-permute-start | bytes 98312 | tf_op jit(solution)/shard_map/ppermute | solution.py:15
  301.6 5.3 %collective-permute-start.21 = (bf16[256,1,64]{0,2,1:T(8,128)(2,1)S(1)}, bf16[256,1,64]{0,2,1:T(8,128)(2,1)S(1)}, u32[]{:S(2)}, u32[]{:S(2)}) collective-permute-start(bf16[256,1,64]{0,2,1:T(8,128)(2,1)S(1)} %get-tuple-element.111), channel_id=1, source_target_pairs={{2,0},{4,2},{6,4},{8,6},{10,8},{12,10},{14,12},{3,1},{5,3},{7,5},{... | collective-permute-start | bytes 98312 | tf_op jit(solution)/shard_map/ppermute | solution.py:18
  306.9 5.5 %collective-permute-start.22 = (bf16[256,6,1]{0,2,1:T(2,128)(2,1)S(1)}, bf16[256,6,1]{0,2,1:T(2,128)(2,1)S(1)}, u32[]{:S(2)}, u32[]{:S(2)}) collective-permute-start(bf16[256,6,1]{0,2,1:T(2,128)(2,1)S(1)} %get-tuple-element.108), channel_id=1, source_target_pairs={{0,1},{2,3},{4,5},{6,7},{8,9},{10,11},{12,13},{14,15},{16,17},{18,... | collective-permute-start | bytes 9224 | tf_op jit(solution)/shard_map/ppermute | solution.py:15
  308.2 4.2 %collective-permute-start.23 = (bf16[256,6,1]{0,2,1:T(2,128)(2,1)S(1)}, bf16[256,6,1]{0,2,1:T(2,128)(2,1)S(1)}, u32[]{:S(2)}, u32[]{:S(2)}) collective-permute-start(bf16[256,6,1]{0,2,1:T(2,128)(2,1)S(1)} %get-tuple-element.109), channel_id=1, source_target_pairs={{1,0},{3,2},{5,4},{7,6},{9,8},{11,10},{13,12},{15,14},{17,16},{19,... | collective-permute-start | bytes 9224 | tf_op jit(solution)/shard_map/ppermute | solution.py:18
  (18 other events, 69.0 us)
where the time goes:
time: 334 us; the launch traced here: 329 us
  local copies, waits for them, and re-layouts  113 us (34%)
  starting transfers between devices  78.2 us (23%)
  matrix products  44.4 us (13%)
  other arithmetic  38.7 us (12%)
  loops' own time  33.9 us (10%)
  waiting for transfers between devices  19.9 us (6%)
    slice x18, local copies, waits for them, and re-layouts, conv_padded(): padded[:, tap_row:tap_row + stride * rows_out:stride, tap_col:tap_col + s...  50.5 us
    ppermute x12, starting transfers between devices, with_halo(): lax.ppermute(lax.slice_in_dim(block, 0, width, axis=dim), axis, backward)  41.1 us
    another operation x1, loops' own time, on_device(): encoded = lax.map(encode_one, jnp.arange(grouped.shape[2], dtype=jnp.int32))  33.9 us
    dot_general x53, matrix products, conv_padded(): jnp.einsum('oc,chw->ohw', kernel[tap_row, tap_col], window, preferred_ele...  28.6 us
    ppermute x12, starting transfers between devices, with_halo(): lax.ppermute(lax.slice_in_dim(block, block.shape[dim] - width, None, axis...  24.5 us
    another operation x1, other arithmetic, on_device(): bev.at[:, cell_ids.reshape(-1)].max(feature_rows)  23.2 us
    while x64, local copies, waits for them, and re-layouts  21.6 us
    all_to_all x1, waiting for transfers between devices, on_device(): lax.all_to_all(encoded, ('row', 'col'), split_axis=0, concat_axis=0, tile...  14.1 us
  transfers between devices with their start and end apart: 26, of which 8 were waited for; matrix products, arithmetic and copies ran while one was open for 26% of the time, Pallas kernels for 0%

commit v1 on v0

v1 whole, which is shorter than its diff:
```python
import functools

import jax
import jax.numpy as jnp
from jax import lax
from jax.experimental import pallas as pl
from jax.experimental.pallas import tpu as pltpu
from jax.sharding import PartitionSpec as P

ROWS_DEV = 16
COLS_DEV = 256
PACK = 4
HALF = 16
LANES = 4


def with_halo(block, sides, before, after):
    for axis, dim in sides:
        count = lax.axis_size(axis)
        forward = [(i, i + 1) for i in range(count - 1)]
        backward = [(target, source) for source, target in forward]
        size = block.shape[dim]
        low = lax.ppermute(lax.slice_in_dim(block, size - before, size, axis=dim), axis, forward)
        high = lax.ppermute(lax.slice_in_dim(block, 0, after, axis=dim), axis, backward)
        block = jnp.concatenate([low, block, high], axis=dim)
    return block


def encode_kernel(tiles, x_ref, meta_ref, w1_ref, w2_ref, b1_ref, b2_ref, out_ref):
    chan = b2_ref.shape[0]
    cap = meta_ref.shape[2]
    points = x_ref.shape[1]
    feat = x_ref.shape[0]
    for t in range(tiles):
        count = meta_ref[t, 0:1, :]
        best = jnp.full((chan, cap), -jnp.inf, jnp.float32)
        for h in range(points // HALF):
            block = x_ref[:, h * HALF : (h + 1) * HALF, t * cap : (t + 1) * cap]
            block = block.reshape(feat * HALF, cap)
            for q in range(HALF // PACK):
                hidden = jnp.dot(w1_ref[q], block, preferred_element_type=jnp.float32)
                hidden = jnp.maximum(hidden + b1_ref[...], 0.0).astype(jnp.bfloat16)
                second = jnp.dot(w2_ref[...], hidden, preferred_element_type=jnp.float32)
                for p in range(PACK):
                    j = h * HALF + q * PACK + p
                    part = second[p * chan : (p + 1) * chan]
                    best = jnp.maximum(best, jnp.where(count > j, part, -jnp.inf))
        vec = jnp.maximum(best + b2_ref[...], 0.0)
        out_ref[t, 0:chan, :] = vec.astype(jnp.bfloat16)
        which = lax.broadcasted_iota(jnp.int32, (16, cap), 0)
        row = jnp.broadcast_to(meta_ref[t, 1:2, :], (16, cap))
        col = jnp.broadcast_to(meta_ref[t, 2:3, :], (16, cap))
        tail = jnp.where(which == 0, row, jnp.where(which == 1, col, 0))
        out_ref[t, chan : chan + 16, :] = tail.astype(jnp.float32).astype(jnp.bfloat16)


def encode_all(points, meta, embed, mix, b_embed, b_mix):
    feat, point_num, slots = points.shape
    tiles, _, cap = meta.shape
    chan = mix.shape[0]
    mid = embed.shape[0]
    groups = HALF // PACK
    pick = (
        jnp.arange(HALF)[None, None, :]
        == PACK * jnp.arange(groups)[:, None, None] + jnp.arange(PACK)[None, :, None]
    )
    w1 = jnp.where(pick[:, :, None, None, :], embed[None, None, :, :, None], 0)
    w1 = w1.reshape(groups, PACK * mid, feat * HALF).astype(jnp.bfloat16)
    eye = jnp.eye(PACK, dtype=jnp.bool_)
    w2 = jnp.where(eye[:, None, :, None], mix[None, :, None, :], 0)
    w2 = w2.reshape(PACK * chan, PACK * mid).astype(jnp.bfloat16)
    b1 = jnp.tile(b_embed, PACK)[:, None]
    b2 = b_mix[:, None]
    step = 2
    return pl.pallas_call(
        functools.partial(encode_kernel, step),
        grid=(tiles // step,),
        in_specs=[
            pl.BlockSpec((feat, point_num, step * cap), lambda i: (0, 0, i)),
            pl.BlockSpec((step, 8, cap), lambda i: (i, 0, 0)),
            pl.BlockSpec(w1.shape, lambda i: (0, 0, 0)),
            pl.BlockSpec(w2.shape, lambda i: (0, 0)),
            pl.BlockSpec(b1.shape, lambda i: (0, 0)),
            pl.BlockSpec(b2.shape, lambda i: (0, 0)),
        ],
        out_specs=pl.BlockSpec((step, chan + 16, cap), lambda i: (i, 0, 0)),
        out_shape=jax.ShapeDtypeStruct((tiles, chan + 16, cap), jnp.bfloat16),
        name="encode",
    )(points, meta, w1, w2, b1, b2)


def scatter_kernel(cell_ref, vec_ref, out_ref, stage, *grids):
    tiles, _, cap = vec_ref.shape
    chan = out_ref.shape[1]
    for grid in grids:
        grid[...] = jnp.zeros_like(grid)

    def per_tile(t, carry):
        stage[...] = vec_ref[t, 0:chan, :].astype(jnp.float32).T
        unroll = 8

        def per_slot(s, inner):
            for k in range(unroll):
                cells = [cell_ref[t * cap + (s * unroll + k) * LANES + a] for a in range(LANES)]
                base = (s * unroll + k) * LANES
                olds = [grids[a][pl.ds(cells[a], 1), :] for a in range(LANES)]
                for a in range(LANES):
                    grids[a][pl.ds(cells[a], 1), :] = jnp.maximum(
                        olds[a], stage[pl.ds(base + a, 1), :]
                    )
            return inner

        return lax.fori_loop(0, cap // (LANES * unroll), per_slot, carry)

    lax.fori_loop(0, tiles, per_tile, 0)
    total = grids[0][...]
    for grid in grids[1:]:
        total = jnp.maximum(total, grid[...])
    out_ref[...] = total.astype(jnp.bfloat16)


def scatter_max(cells, vectors, chan):
    tiles, _, cap = vectors.shape
    area = ROWS_DEV * COLS_DEV
    return pl.pallas_call(
        scatter_kernel,
        in_specs=[
            pl.BlockSpec(memory_space=pltpu.SMEM),
            pl.BlockSpec(memory_space=pltpu.VMEM),
        ],
        out_specs=pl.BlockSpec(memory_space=pltpu.VMEM),
        out_shape=jax.ShapeDtypeStruct((area, chan), jnp.bfloat16),
        scratch_shapes=[pltpu.VMEM((cap, chan), jnp.float32)]
        + [pltpu.VMEM((area, chan), jnp.float32)] * LANES,
        name="scatter_max",
    )(cells, vectors)


def conv_valid(padded, kernel, bias_vec, stride):
    summed = lax.conv_general_dilated(
        padded[None],
        jnp.swapaxes(kernel, 2, 3),
        (stride, stride),
        "VALID",
        dimension_numbers=("NHWC", "HWIO", "NHWC"),
        preferred_element_type=jnp.float32,
    )[0]
    return jax.nn.relu(summed + bias_vec).astype(jnp.bfloat16)


def inside(block, edge):
    rows, cols, _ = block.shape
    own = (rows - 2 * edge, cols - 2 * edge)
    keep = None
    for dim, axis in enumerate(("row", "col")):
        place = lax.broadcasted_iota(jnp.int32, (rows, cols, 1), dim) - edge
        place = place + lax.axis_index(axis) * own[dim]
        good = (place >= 0) & (place < own[dim] * lax.axis_size(axis))
        keep = good if keep is None else keep & good
    return jnp.where(keep, block, jnp.zeros((), block.dtype))


def lift_layer(inputs, kernel, bias_vec):
    factor = kernel.shape[0]
    rows, cols, chan = inputs.shape
    if factor > 1:
        eye = jnp.eye(factor, dtype=jnp.bool_)
        wide = jnp.where(
            eye[None, None, :, :, None], inputs[:, :, None, None, :], jnp.zeros((), inputs.dtype)
        )
        wide = wide.reshape(rows, cols * factor, factor * chan)
    else:
        wide = inputs
    weight = jnp.transpose(kernel, (2, 0, 1, 3)).reshape(kernel.shape[2], factor, factor * chan)
    product = jnp.einsum("oak,ijk->oiaj", weight, wide, preferred_element_type=jnp.float32)
    product = product.reshape(kernel.shape[2], rows * factor, cols * factor)
    return jax.nn.relu(product + bias_vec[:, None, None]).astype(jnp.bfloat16)


def on_device(
    points,
    pillar_cell,
    point_count,
    tile_count,
    point_embed,
    point_mix,
    first_conv,
    second_conv,
    third_conv,
    fourth_conv,
    fifth_conv,
    sixth_conv,
    near_lift,
    mid_lift,
    far_lift,
    biases,
):
    extents = [
        point_embed.shape[0],
        point_mix.shape[0],
        first_conv.shape[2],
        second_conv.shape[2],
        third_conv.shape[2],
        fourth_conv.shape[2],
        fifth_conv.shape[2],
        sixth_conv.shape[2],
        near_lift.shape[2],
        mid_lift.shape[2],
        far_lift.shape[2],
    ]
    pieces = []
    offset = 0
    for extent in extents:
        pieces.append(biases[offset : offset + extent])
        offset += extent
    tile_num = tile_count.shape[0]
    capacity = points.shape[2] // tile_num
    ncols_all = COLS_DEV * lax.axis_size("col")
    live_slot = lax.broadcasted_iota(jnp.int32, (tile_num, capacity), 1) < tile_count[:, None]
    live_points = jnp.where(live_slot, point_count.reshape(tile_num, capacity), 0)
    row_local = (pillar_cell // ncols_all % ROWS_DEV).reshape(tile_num, capacity)
    col_local = (pillar_cell % COLS_DEV).reshape(tile_num, capacity)
    which = lax.broadcasted_iota(jnp.int32, (1, 8, 1), 1)
    meta = jnp.where(
        which == 0,
        live_points[:, None, :],
        jnp.where(which == 1, row_local[:, None, :], col_local[:, None, :]),
    )
    encoded = encode_all(points, meta, point_embed, point_mix, pieces[0], pieces[1])
    vectors = lax.all_to_all(encoded, ("row", "col"), split_axis=0, concat_axis=0, tiled=True)
    chan = point_mix.shape[0]
    place = vectors[:, chan : chan + 2, :].astype(jnp.int32)
    cells = (place[:, 0] * COLS_DEV + place[:, 1]).reshape(-1)
    bev = scatter_max(cells, vectors, chan).reshape(ROWS_DEV, COLS_DEV, chan)
    sides = (("row", 0), ("col", 1))
    level_one_a = inside(conv_valid(with_halo(bev, sides, 2, 2), first_conv, pieces[2], 1), 1)
    level_one = conv_valid(level_one_a, second_conv, pieces[3], 1)
    level_two_a = inside(conv_valid(with_halo(level_one, sides, 3, 2), third_conv, pieces[4], 2), 1)
    level_two = conv_valid(level_two_a, fourth_conv, pieces[5], 1)
    level_three_a = inside(
        conv_valid(with_halo(level_two, sides, 3, 2), fifth_conv, pieces[6], 2), 1
    )
    level_three = conv_valid(level_three_a, sixth_conv, pieces[7], 1)
    near = lift_layer(level_one, near_lift, pieces[8])
    middle = lift_layer(level_two, mid_lift, pieces[9])
    distant = lift_layer(level_three, far_lift, pieces[10])
    return jnp.concatenate([near, middle, distant], axis=0)


def solution(mesh):
    return jax.shard_map(
        on_device,
        mesh=mesh,
        in_specs=(
            P(None, None, ("slab", "row", "col")),
            P(("slab", "row", "col")),
            P(("slab", "row", "col")),
            P(("slab", "row", "col")),
            P(),
            P(),
            P(),
            P(),
            P(),
            P(),
            P(),
            P(),
            P(),
            P(),
            P(),
            P(),
        ),
        out_specs=P(None, ("slab", "row"), "col"),
        check_vma=False,
    )
```

time: 334 us -> 170 us (0.51); the launches traced: 329 us -> 169 us
  local copies, waits for them, and re-layouts: 113 us -> 46.6 us
  starting transfers between devices: 78.2 us -> 39.8 us
  loops' own time: 33.9 us -> 0 us
  matrix products: 44.4 us -> 15.4 us
  Pallas kernels: 0 us -> 23.5 us
  other arithmetic: 38.7 us -> 19.3 us
  waiting for transfers between devices: 19.9 us -> 23.5 us
    slice x28 -> x7, local copies, waits for them, and re-layouts: 51 us -> 3.54 us  [the longest x4 2.1 us: with_halo(): lax.slice_in_dim(block, size - before, size, axis=dim)]
    dot_general x72 -> x3, matrix products: 44.4 us -> 6.02 us  [lift_layer(): jnp.einsum('oak,ijk->oiaj', weight, wide, preferred_element_type=jnp.floa...]
    another operation x1 -> x0, loops' own time: 33.9 us -> none  [on_device(): encoded = lax.map(encode_one, jnp.arange(grouped.shape[2], dtype=jnp.int32))]
    ppermute x24 -> x12, starting transfers between devices: 65.6 us -> 33.2 us  [the longest x6 22.5 us: with_halo(): lax.ppermute(lax.slice_in_dim(block, 0, after, axis=dim), axis, backward)]
    pallas_call x0 -> x2, Pallas kernels: none -> 23.5 us  [the longest x1 13.4 us: encode_all(): pl.pallas_call(functools.partial(encode_kernel, step), grid=(tiles // ste...]
    another operation x1 -> x0, other arithmetic: 23.2 us -> none  [on_device(): bev.at[:, cell_ids.reshape(-1)].max(feature_rows)]
    while x64 -> x0, local copies, waits for them, and re-layouts: 21.6 us -> none
    conv_general_dilated x0 -> x19, local copies, waits for them, and re-layouts: none -> 13.4 us  [conv_valid(): lax.conv_general_dilated(padded[None], jnp.swapaxes(kernel, 2, 3), (strid...]
  transfers between devices with their start and end apart: 26 -> 13, of which waited for: 8 -> 5; matrix products, arithmetic and copies ran while one was open for 26% -> 10% of each run, Pallas kernels for 0% -> 0%
where the time goes in v1:
time: 170 us; the launch traced here: 169 us
  local copies, waits for them, and re-layouts  46.6 us (27%)
  starting transfers between devices  39.8 us (23%)
  Pallas kernels  23.5 us (14%)
  waiting for transfers between devices  23.5 us (14%)
  other arithmetic  19.3 us (11%)
  matrix products  15.4 us (9%)
    ppermute x6, starting transfers between devices, with_halo(): lax.ppermute(lax.slice_in_dim(block, 0, after, axis=dim), axis, backward)  22.5 us
    all_to_all x1, waiting for transfers between devices, on_device(): lax.all_to_all(encoded, ('row', 'col'), split_axis=0, concat_axis=0, tile...  14.3 us
    pallas_call x1, Pallas kernels, encode_all(): pl.pallas_call(functools.partial(encode_kernel, step), grid=(tiles // ste...  13.4 us
    conv_general_dilated x19, local copies, waits for them, and re-layouts, conv_valid(): lax.conv_general_dilated(padded[None], jnp.swapaxes(kernel, 2, 3), (strid...  13.4 us
    ppermute x6, starting transfers between devices, with_halo(): lax.ppermute(lax.slice_in_dim(block, size - before, size, axis=dim), axis...  10.7 us
    pallas_call x1, Pallas kernels, scatter_max(): pl.pallas_call(scatter_kernel, in_specs=[pl.BlockSpec(memory_space=pltpu....  10 us
    conv_general_dilated x6, matrix products, conv_valid(): lax.conv_general_dilated(padded[None], jnp.swapaxes(kernel, 2, 3), (strid...  9.39 us
    ppermute x6, waiting for transfers between devices, with_halo(): lax.ppermute(lax.slice_in_dim(block, 0, after, axis=dim), axis, backward)  7.27 us
  transfers between devices with their start and end apart: 13, of which 5 were waited for; matrix products, arithmetic and copies ran while one was open for 10% of the time, Pallas kernels for 0%

profile of v1, /device:TPU:9, one launch (start us, length us, event | category | flops | bytes accessed | tf_op | source)
XLA Modules:
  0.0 169.1 jit_solution(2295773670401483829)
XLA Ops:
  1.6 1.5 fusion.113
  9.6 13.4 %encode.1 = bf16[16,80,256]{2,1,0:T(8,128)(2,1)} custom-call(bf16[9,32,4096]{2,1,0:T(8,128)(2,1)} %x_ref.1, s32[16,8,256]{2,1,0:T(8,128)} %select_select_fusion.meta_ref, bf16[4,256,144]{2,1,0:T(8,128)(2,1)} %broadcast_select_fusion.2.w1_ref, bf16[256,256]{1,0:T(8,128)(2,1)} %select_n.96.w2_ref, f32[256,1]{1,0:T(8,128)} %broadcast_in_dim_tile.4.b1_ref, ...), custom_call_target="tpu_custom_call" | custom-call | tf_op jit(solution)/shard_map/encode/pallas_call | solution.py:75
  23.1 6.6 %all-to-all-start = ((bf16[16,80,256]{2,1,0:T(8,128)(2,1)}), bf16[16,80,256]{2,1,0:T(8,128)(2,1)S(1)}, u32[]{:S(2)}, u32[]{:S(2)}) async-start(bf16[16,80,256]{2,1,0:T(8,128)(2,1)} %encode.1), calls=%async_computation | async-start | bytes 1310720 | tf_op jit(solution)/shard_map/all_to_all | solution.py:230
  32.3 14.3 %all-to-all-done.vec_ref = bf16[16,80,256]{2,1,0:T(8,128)(2,1)S(1)} async-done(((bf16[16,80,256]{2,1,0:T(8,128)(2,1)}), bf16[16,80,256]{2,1,0:T(8,128)(2,1)S(1)}, u32[]{:S(2)}, u32[]{:S(2)}) %all-to-all-start) | async-done | bytes 655392 | tf_op jit(solution)/shard_map/all_to_all | solution.py:230
  47.4 10.0 %scatter_max.1 = bf16[4096,64]{1,0:T(8,128)(2,1)} custom-call(s32[4096]{0:T(1024)} %bitcast.162, bf16[16,80,256]{2,1,0:T(8,128)(2,1)} %copy-done.3), custom_call_target="tpu_custom_call" | custom-call | tf_op jit(solution)/shard_map/scatter_max/pallas_call | solution.py:125
  58.6 2.6 %collective-permute-start = (bf16[2,256,64]{2,1,0:T(8,128)(2,1)S(1)}, bf16[2,256,64]{2,1,0:T(8,128)(2,1)S(1)}, u32[]{:S(2)}, u32[]{:S(2)}) collective-permute-start(bf16[2,256,64]{2,1,0:T(8,128)(2,1)S(1)} %bitcast.161), channel_id=1, source_target_pairs={{0,2},{2,4},{4,6},{6,8},{8,10},{10,12},{12,14},{1,3},{3,5},{5,7},{... | collective-permute-start | bytes 196616 | tf_op jit(solution)/shard_map/ppermute | solution.py:23
  61.2 3.6 %collective-permute-start.1 = (bf16[2,256,64]{2,1,0:T(8,128)(2,1)S(1)}, bf16[2,256,64]{2,1,0:T(8,128)(2,1)S(1)}, u32[]{:S(2)}, u32[]{:S(2)}) collective-permute-start(bf16[2,256,64]{2,1,0:T(8,128)(2,1)S(1)} %bitcast.160), channel_id=1, source_target_pairs={{2,0},{4,2},{6,4},{8,6},{10,8},{12,10},{14,12},{3,1},{5,3},{7,5},{... | collective-permute-start | bytes 196616 | tf_op jit(solution)/shard_map/ppermute | solution.py:24
  64.8 2.0 %collective-permute-done = bf16[2,256,64]{2,1,0:T(8,128)(2,1)S(1)} collective-permute-done((bf16[2,256,64]{2,1,0:T(8,128)(2,1)S(1)}, bf16[2,256,64]{2,1,0:T(8,128)(2,1)S(1)}, u32[]{:S(2)}, u32[]{:S(2)}) %collective-permute-start) | collective-permute-done | bytes 65568 | tf_op jit(solution)/shard_map/ppermute | solution.py:23
  66.7 2.9 %collective-permute-done.1 = bf16[2,256,64]{2,1,0:T(8,128)(2,1)S(1)} collective-permute-done((bf16[2,256,64]{2,1,0:T(8,128)(2,1)S(1)}, bf16[2,256,64]{2,1,0:T(8,128)(2,1)S(1)}, u32[]{:S(2)}, u32[]{:S(2)}) %collective-permute-start.1) | collective-permute-done | bytes 65568 | tf_op jit(solution)/shard_map/ppermute | solution.py:24
  69.6 1.4 pad_maximum_fusion.5
  72.3 4.2 %collective-permute-start.3 = (bf16[20,2,64]{2,1,0:T(2,128)(2,1)}, bf16[20,2,64]{2,1,0:T(2,128)(2,1)}, u32[]{:S(2)}, u32[]{:S(2)}) collective-permute-start(bf16[20,2,64]{2,1,0:T(2,128)(2,1)} %get-tuple-element.6), channel_id=1, source_target_pairs={{1,0},{3,2},{5,4},{7,6},{9,8},{11,10},{13,12},{15,14},{17,16},{19,... | collective-permute-start | bytes 15368 | tf_op jit(solution)/shard_map/ppermute | solution.py:24
  78.6 1.7 copy.76
  82.8 2.4 %reshape.302 = bf16[20,1,8,33,64]{4,3,2,0,1:T(8,128)(2,1)S(1)} reshape(bf16[20,1,264,64]{3,2,0,1:T(8,128)(2,1)} %pad) | data formatting | bytes 1351680 | tf_op jit(solution)/shard_map/conv_general_dilated | solution.py:140
  86.1 3.0 %maximum_convert_fusion = bf16[18,8,33,64]{3,1,2,0:T(8,128)(2,1)S(1)} fusion(bf16[3,3,64,64]{3,2,1,0:T(8,128)(2,1)S(1)} %copy-done.23, bf16[20,1,7,2,64]{4,2,3,0,1:T(8,128)(2,1)S(1)} %slice.130, bf16[20,1,8,33,64]{4,2,3,0,1:T(8,128)(2,1)S(1)} %copy.58, f32[64]{0:T(128)S(1)} %copy-done.20, pred[8,33]{0,1:T(8,128)(4,1)S(1)} %copy-done.28), kind=kOutput, calls=%fused_computation.7 | convolution fusion | flops 353722368 | bytes 1394184 | tf_op jit(solution)/shard_map/conv_general_dilated | solution.py:140
  90.7 2.6 %slice_select_fusion = bf16[18,1,258,64]{3,2,0,1:T(8,128)(2,1)S(1)} fusion(bf16[18,1,264,64]{3,2,0,1:T(8,128)(2,1)} %reshape.306, pred[18,258]{1,0:T(8,128)(4,1)S(1)} %broadcast_and_fusion.1), kind=kLoop, calls=%fused_computation.49 | loop fusion | flops 297216 | bytes 1193508 | tf_op jit(solution)/shard_map/jit(_where)/select_n | solution.py:160
  94.6 2.3 %reshape.309 = bf16[18,1,8,33,64]{4,3,2,0,1:T(8,128)(2,1)S(1)} reshape(bf16[18,1,264,64]{3,2,0,1:T(8,128)(2,1)} %pad.2) | data formatting | bytes 1216512 | tf_op jit(solution)/shard_map/conv_general_dilated | solution.py:140
  97.2 3.8 %maximum_convert_fusion.1 = (bf16[16,8,33,64]{3,1,2,0:T(8,128)(2,1)}, f32[16,8,33,64]{3,1,2,0:T(8,128)S(1)}) fusion(f32[64]{0:T(128)S(1)} %copy-done.15, bf16[3,3,64,64]{3,2,1,0:T(8,128)(2,1)S(1)} %copy-done.24, bf16[18,1,7,2,64]{4,2,3,0,1:T(8,128)(2,1)S(1)} %slice.132, bf16[18,1,8,33,64]{4,2,3,0,1:T(8,128)(2,1)S(1)} %copy.61, pred[8,33]{0,1:T(8,128)(4,1)S(1)} %copy-done.27), kind=kOutput, calls=%fused_computation.8 | convolution fusion | flops 314443776 | bytes 2336776 | tf_op jit(solution)/shard_map/conv_general_dilated | solution.py:140
  102.4 2.2 %collective-permute-start.4 = (bf16[3,256,64]{2,0,1:T(4,128)(2,1)S(1)}, bf16[3,256,64]{2,0,1:T(4,128)(2,1)}, u32[]{:S(2)}, u32[]{:S(2)}) collective-permute-start(bf16[3,256,64]{2,0,1:T(4,128)(2,1)S(1)} %slice.135), channel_id=1, source_target_pairs={{0,2},{2,4},{4,6},{6,8},{8,10},{10,12},{12,14},{1,3},{3,5},{5,7},{... | collective-permute-start | bytes 294920 | tf_op jit(solution)/shard_map/ppermute | solution.py:23
  104.7 4.2 %collective-permute-start.5 = (bf16[2,256,64]{2,0,1:T(2,128)(2,1)}, bf16[2,256,64]{2,0,1:T(2,128)(2,1)}, u32[]{:S(2)}, u32[]{:S(2)}) collective-permute-start(bf16[2,256,64]{2,0,1:T(2,128)(2,1)} %slice.136), channel_id=1, source_target_pairs={{2,0},{4,2},{6,4},{8,6},{10,8},{12,10},{14,12},{3,1},{5,3},{7,5},{... | collective-permute-start | bytes 196616 | tf_op jit(solution)/shard_map/ppermute | solution.py:24
  109.7 1.4 copy.62
  112.1 3.7 %collective-permute-done.5 = bf16[2,256,64]{2,0,1:T(2,128)(2,1)} collective-permute-done((bf16[2,256,64]{2,0,1:T(2,128)(2,1)}, bf16[2,256,64]{2,0,1:T(2,128)(2,1)}, u32[]{:S(2)}, u32[]{:S(2)}) %collective-permute-start.5) | collective-permute-done | bytes 65568 | tf_op jit(solution)/shard_map/ppermute | solution.py:24
  119.6 3.1 %collective-permute-start.7 = (bf16[21,2,64]{1,2,0:T(8,128)(2,1)S(1)}, bf16[21,2,64]{1,2,0:T(8,128)(2,1)S(1)}, u32[]{:S(2)}, u32[]{:S(2)}) collective-permute-start(bf16[21,2,64]{1,2,0:T(8,128)(2,1)S(1)} %slice.138), channel_id=1, source_target_pairs={{1,0},{3,2},{5,4},{7,6},{9,8},{11,10},{13,12},{15,14},{17,16},{19,... | collective-permute-start | bytes 16136 | tf_op jit(solution)/shard_map/ppermute | solution.py:24
  122.7 1.5 fusion.11
  125.0 3.4 %reshape.393 = bf16[21,1,8,34,64]{3,2,4,0,1:T(8,128)(2,1)} reshape(bf16[21,1,272,64]{2,3,0,1:T(8,128)(2,1)S(1)} %pad.4) | data formatting | bytes 1462272 | tf_op jit(solution)/shard_map/conv_general_dilated | solution.py:140
  128.4 3.8 %copy.70 = bf16[21,1,8,34,64]{4,2,3,0,1:T(8,128)(2,1)S(1)} copy(bf16[21,1,8,34,64]{3,2,4,0,1:T(8,128)(2,1)} %reshape.393) | data formatting | bytes 1462272 | tf_op jit(solution)/shard_map/conv_general_dilated | solution.py:140
  136.5 1.9 %collective-permute-start.8 = (bf16[3,128,128]{2,0,1:T(4,128)(2,1)}, bf16[3,128,128]{2,0,1:T(4,128)(2,1)}, u32[]{:S(2)}, u32[]{:S(2)}) collective-permute-start(bf16[3,128,128]{2,0,1:T(4,128)(2,1)} %slice.143), channel_id=1, source_target_pairs={{0,2},{2,4},{4,6},{6,8},{8,10},{10,12},{12,14},{1,3},{3,5},{5,7},{... | collective-permute-start | bytes 294920 | tf_op jit(solution)/shard_map/ppermute | solution.py:23
  138.4 4.3 %collective-permute-start.9 = (bf16[2,128,128]{2,0,1:T(2,128)(2,1)}, bf16[2,128,128]{2,0,1:T(2,128)(2,1)}, u32[]{:S(2)}, u32[]{:S(2)}) collective-permute-start(bf16[2,128,128]{2,0,1:T(2,128)(2,1)} %slice.144), channel_id=1, source_target_pairs={{2,0},{4,2},{6,4},{8,6},{10,8},{12,10},{14,12},{3,1},{5,3},{7,5},{... | collective-permute-start | bytes 196616 | tf_op jit(solution)/shard_map/ppermute | solution.py:24
  144.4 1.4 fusion.49
  149.2 3.3 %collective-permute-start.11 = (bf16[13,2,128]{2,0,1:T(8,128)(2,1)S(1)}, bf16[13,2,128]{2,0,1:T(8,128)(2,1)S(1)}, u32[]{:S(2)}, u32[]{:S(2)}) collective-permute-start(bf16[13,2,128]{2,0,1:T(8,128)(2,1)S(1)} %pad_maximum_fusion.6), channel_id=1, source_target_pairs={{1,0},{3,2},{5,4},{7,6},{9,8},{11,10},{13,12},{15,14},{17,16},{19,... | collective-permute-start | bytes 19976 | tf_op jit(solution)/shard_map/ppermute | solution.py:24
  158.0 2.7 %reshape.389 = bf16[4,256,1024,1]{2,1,0,3:T(8,128)(2,1)} reshape(bf16[4,64,4,4,256]{4,3,2,1,0:T(4,128)(2,1)S(1)} %broadcast_select_fusion) | data formatting | bytes 4194304 | tf_op jit(solution)/shard_map/jit(_where)/select_n | solution.py:168
  160.7 3.1 %fusion.12 = f32[4,256,128,4]{1,2,3,0:T(8,128)S(1)} fusion(bf16[128,4,1024,1]{0,2,1,3:T(8,128)(2,1)} %bitcast.158, bf16[4,256,1024,1]{2,1,0,3:T(8,128)(2,1)} %reshape.389), kind=kOutput, calls=%fused_computation.22 | convolution fusion | flops 1073741824 | bytes 5242880 | tf_op jit(solution)/shard_map/oak,ijk->oiaj/dot_general | solution.py:175
  165.7 3.4 %copy.88 = bf16[384,16,256]{2,1,0:T(8,128)(2,1)} copy(bf16[384,16,256]{2,0,1:T(8,128)(2,1)S(1)} %pad_maximum_fusion) | data formatting | bytes 6291456 | tf_op jit(solution)/shard_map/concatenate | solution.py:247
  (177 shorter events, 46.5 us)
Async XLA Ops:
  0.0 156.4 %copy-start = (bf16[3,3,256,256]{3,2,1,0:T(8,128)(2,1)S(1)}, bf16[3,3,256,256]{3,2,1,0:T(8,128)(2,1)}, u32[]{:S(2)}) copy-start(bf16[3,3,256,256]{3,2,1,0:T(8,128)(2,1)} %param.27) | copy-start | bytes 3538948
  0.0 7.6 %copy-start.9 = (bf16[64,9]{0,1:T(8,128)(2,1)S(1)}, bf16[64,9]{0,1:T(8,128)(2,1)}, u32[]{:S(2)}) copy-start(bf16[64,9]{0,1:T(8,128)(2,1)} %param.20) | copy-start | bytes 3460
  0.0 8.0 %copy-start.17 = (s32[16]{0:T(128)S(1)}, s32[16]{0:T(128)}, u32[]{:S(2)}) copy-start(s32[16]{0:T(128)} %param.19) | copy-start | bytes 196
  0.0 7.6 %copy-start.10 = (pred[4,4]{1,0:T(4,128)(4,1)}, pred[4,4]{1,0:T(4,128)(4,1)S(1)}, u32[]{:S(2)}) copy-start(pred[4,4]{1,0:T(4,128)(4,1)S(1)} %iota_compare_fusion.8) | copy-start | bytes 52
  9.6 20.7 %copy-start.7 = (f32[1408]{0:T(1024)S(1)}, f32[1408]{0:T(1024)}, u32[]{:S(2)}) copy-start(f32[1408]{0:T(1024)} %param.31) | copy-start | bytes 16900
  23.1 23.5 %all-to-all-start = ((bf16[16,80,256]{2,1,0:T(8,128)(2,1)}), bf16[16,80,256]{2,1,0:T(8,128)(2,1)S(1)}, u32[]{:S(2)}, u32[]{:S(2)}) async-start(bf16[16,80,256]{2,1,0:T(8,128)(2,1)} %encode.1), calls=%async_computation | async-start | bytes 1310720 | tf_op jit(solution)/shard_map/all_to_all | solution.py:230
  29.7 47.6 %copy-start.4 = (bf16[4,4,128,256]{3,2,1,0:T(8,128)(2,1)S(1)}, bf16[4,4,128,256]{3,2,1,0:T(8,128)(2,1)}, u32[]{:S(2)}) copy-start(bf16[4,4,128,256]{3,2,1,0:T(8,128)(2,1)} %param.30) | copy-start | bytes 3145732
  57.5 22.8 %copy-start.1 = (bf16[4096,64]{1,0:T(8,128)(2,1)S(1)}, bf16[4096,64]{1,0:T(8,128)(2,1)}, u32[]{:S(2)}) copy-start(bf16[4096,64]{1,0:T(8,128)(2,1)} %scatter_max.1) | copy-start | bytes 1572868
  58.6 8.2 %collective-permute-start = (bf16[2,256,64]{2,1,0:T(8,128)(2,1)S(1)}, bf16[2,256,64]{2,1,0:T(8,128)(2,1)S(1)}, u32[]{:S(2)}, u32[]{:S(2)}) collective-permute-start(bf16[2,256,64]{2,1,0:T(8,128)(2,1)S(1)} %bitcast.161), channel_id=1, source_target_pairs={{0,2},{2,4},{4,6},{6,8},{8,10},{10,12},{12,14},{1,3},{3,5},{5,7},{... | collective-permute-start | bytes 196616 | tf_op jit(solution)/shard_map/ppermute | solution.py:23
  61.2 8.4 %collective-permute-start.1 = (bf16[2,256,64]{2,1,0:T(8,128)(2,1)S(1)}, bf16[2,256,64]{2,1,0:T(8,128)(2,1)S(1)}, u32[]{:S(2)}, u32[]{:S(2)}) collective-permute-start(bf16[2,256,64]{2,1,0:T(8,128)(2,1)S(1)} %bitcast.160), channel_id=1, source_target_pairs={{2,0},{4,2},{6,4},{8,6},{10,8},{12,10},{14,12},{3,1},{5,3},{7,5},{... | collective-permute-start | bytes 196616 | tf_op jit(solution)/shard_map/ppermute | solution.py:24
  71.0 9.2 %collective-permute-start.2 = (bf16[20,2,64]{2,1,0:T(2,128)(2,1)}, bf16[20,2,64]{2,1,0:T(2,128)(2,1)}, u32[]{:S(2)}, u32[]{:S(2)}) collective-permute-start(bf16[20,2,64]{2,1,0:T(2,128)(2,1)} %get-tuple-element.5), channel_id=1, source_target_pairs={{0,1},{2,3},{4,5},{6,7},{8,9},{10,11},{12,13},{14,15},{16,17},{18,... | collective-permute-start | bytes 15368 | tf_op jit(solution)/shard_map/ppermute | solution.py:23
  72.3 7.9 %collective-permute-start.3 = (bf16[20,2,64]{2,1,0:T(2,128)(2,1)}, bf16[20,2,64]{2,1,0:T(2,128)(2,1)}, u32[]{:S(2)}, u32[]{:S(2)}) collective-permute-start(bf16[20,2,64]{2,1,0:T(2,128)(2,1)} %get-tuple-element.6), channel_id=1, source_target_pairs={{1,0},{3,2},{5,4},{7,6},{9,8},{11,10},{13,12},{15,14},{17,16},{19,... | collective-permute-start | bytes 15368 | tf_op jit(solution)/shard_map/ppermute | solution.py:24
  94.6 2.5 %copy-start.15 = (f32[64]{0:T(128)S(1)}, f32[64]{0:T(128)}, u32[]{:S(2)}) copy-start(f32[64]{0:T(128)} %get-tuple-element.18) | copy-start | bytes 772
  94.6 2.5 %copy-start.24 = (bf16[3,3,64,64]{3,2,1,0:T(8,128)(2,1)S(1)}, bf16[3,3,64,64]{3,2,1,0:T(8,128)(2,1)}, u32[]{:S(2)}) copy-start(bf16[3,3,64,64]{3,2,1,0:T(8,128)(2,1)} %param.23) | copy-start | bytes 221188
  94.6 2.5 %copy-start.27 = (pred[8,33]{0,1:T(8,128)(4,1)S(1)}, pred[8,33]{0,1:T(8,128)(4,1)}, u32[]{:S(2)}) copy-start(pred[8,33]{0,1:T(8,128)(4,1)} %constant.127) | copy-start | bytes 796
  102.4 14.4 %collective-permute-start.4 = (bf16[3,256,64]{2,0,1:T(4,128)(2,1)S(1)}, bf16[3,256,64]{2,0,1:T(4,128)(2,1)}, u32[]{:S(2)}, u32[]{:S(2)}) collective-permute-start(bf16[3,256,64]{2,0,1:T(4,128)(2,1)S(1)} %slice.135), channel_id=1, source_target_pairs={{0,2},{2,4},{4,6},{6,8},{8,10},{10,12},{12,14},{1,3},{3,5},{5,7},{... | collective-permute-start | bytes 294920 | tf_op jit(solution)/shard_map/ppermute | solution.py:23
  104.7 11.2 %collective-permute-start.5 = (bf16[2,256,64]{2,0,1:T(2,128)(2,1)}, bf16[2,256,64]{2,0,1:T(2,128)(2,1)}, u32[]{:S(2)}, u32[]{:S(2)}) collective-permute-start(bf16[2,256,64]{2,0,1:T(2,128)(2,1)} %slice.136), channel_id=1, source_target_pairs={{2,0},{4,2},{6,4},{8,6},{10,8},{12,10},{14,12},{3,1},{5,3},{7,5},{... | collective-permute-start | bytes 196616 | tf_op jit(solution)/shard_map/ppermute | solution.py:24
  111.3 11.4 %copy-start.19 = (f32[128]{0:T(128)S(1)}, f32[128]{0:T(128)}, u32[]{:S(2)}) copy-start(f32[128]{0:T(128)} %get-tuple-element.11) | copy-start | bytes 1540
  112.1 10.6 %copy-start.26 = (bf16[1,1,128,64]{2,3,1,0:T(8,128)(2,1)S(1)}, bf16[1,1,128,64]{2,3,1,0:T(8,128)(2,1)}, u32[]{:S(2)}) copy-start(bf16[1,1,128,64]{2,3,1,0:T(8,128)(2,1)} %param.28) | copy-start | bytes 49156
  118.3 5.9 %collective-permute-start.6 = (bf16[21,3,64]{1,2,0:T(8,128)(2,1)S(1)}, bf16[21,3,64]{1,2,0:T(8,128)(2,1)S(1)}, u32[]{:S(2)}, u32[]{:S(2)}) collective-permute-start(bf16[21,3,64]{1,2,0:T(8,128)(2,1)S(1)} %slice.137), channel_id=1, source_target_pairs={{0,1},{2,3},{4,5},{6,7},{8,9},{10,11},{12,13},{14,15},{16,17},{18,... | collective-permute-start | bytes 24200 | tf_op jit(solution)/shard_map/ppermute | solution.py:23
  119.6 4.6 %collective-permute-start.7 = (bf16[21,2,64]{1,2,0:T(8,128)(2,1)S(1)}, bf16[21,2,64]{1,2,0:T(8,128)(2,1)S(1)}, u32[]{:S(2)}, u32[]{:S(2)}) collective-permute-start(bf16[21,2,64]{1,2,0:T(8,128)(2,1)S(1)} %slice.138), channel_id=1, source_target_pairs={{1,0},{3,2},{5,4},{7,6},{9,8},{11,10},{13,12},{15,14},{17,16},{19,... | collective-permute-start | bytes 16136 | tf_op jit(solution)/shard_map/ppermute | solution.py:24
  128.4 3.9 %copy-start.18 = (f32[128]{0:T(128)S(1)}, f32[128]{0:T(128)}, u32[]{:S(2)}) copy-start(f32[128]{0:T(128)} %get-tuple-element.14) | copy-start | bytes 1540
  128.4 3.9 %copy-start.25 = (bf16[3,3,128,64]{2,3,1,0:T(8,128)(2,1)S(1)}, bf16[3,3,128,64]{2,3,1,0:T(8,128)(2,1)}, u32[]{:S(2)}) copy-start(bf16[3,3,128,64]{2,3,1,0:T(8,128)(2,1)} %param.24) | copy-start | bytes 442372
  128.4 3.9 %copy-start.30 = (pred[8,17]{0,1:T(8,128)(4,1)S(1)}, pred[8,17]{0,1:T(8,128)(4,1)}, u32[]{:S(2)}) copy-start(pred[8,17]{0,1:T(8,128)(4,1)} %constant.130) | copy-start | bytes 412
  136.5 10.0 %collective-permute-start.8 = (bf16[3,128,128]{2,0,1:T(4,128)(2,1)}, bf16[3,128,128]{2,0,1:T(4,128)(2,1)}, u32[]{:S(2)}, u32[]{:S(2)}) collective-permute-start(bf16[3,128,128]{2,0,1:T(4,128)(2,1)} %slice.143), channel_id=1, source_target_pairs={{0,2},{2,4},{4,6},{6,8},{8,10},{10,12},{12,14},{1,3},{3,5},{5,7},{... | collective-permute-start | bytes 294920 | tf_op jit(solution)/shard_map/ppermute | solution.py:23
  138.4 8.0 %collective-permute-start.9 = (bf16[2,128,128]{2,0,1:T(2,128)(2,1)}, bf16[2,128,128]{2,0,1:T(2,128)(2,1)}, u32[]{:S(2)}, u32[]{:S(2)}) collective-permute-start(bf16[2,128,128]{2,0,1:T(2,128)(2,1)} %slice.144), channel_id=1, source_target_pairs={{2,0},{4,2},{6,4},{8,6},{10,8},{12,10},{14,12},{3,1},{5,3},{7,5},{... | collective-permute-start | bytes 196616 | tf_op jit(solution)/shard_map/ppermute | solution.py:24
  144.4 8.0 %copy-start.14 = (f32[128]{0:T(128)S(1)}, f32[128]{0:T(128)}, u32[]{:S(2)}) copy-start(f32[128]{0:T(128)} %get-tuple-element.12) | copy-start | bytes 1540
  147.2 6.6 %collective-permute-start.10 = (bf16[13,3,128]{2,0,1:T(8,128)(2,1)S(1)}, bf16[13,3,128]{2,0,1:T(8,128)(2,1)S(1)}, u32[]{:S(2)}, u32[]{:S(2)}) collective-permute-start(bf16[13,3,128]{2,0,1:T(8,128)(2,1)S(1)} %pad_maximum_fusion.2), channel_id=1, source_target_pairs={{0,1},{2,3},{4,5},{6,7},{8,9},{10,11},{12,13},{14,15},{16,17},{18,... | collective-permute-start | bytes 29960 | tf_op jit(solution)/shard_map/ppermute | solution.py:23
  149.2 4.6 %collective-permute-start.11 = (bf16[13,2,128]{2,0,1:T(8,128)(2,1)S(1)}, bf16[13,2,128]{2,0,1:T(8,128)(2,1)S(1)}, u32[]{:S(2)}, u32[]{:S(2)}) collective-permute-start(bf16[13,2,128]{2,0,1:T(8,128)(2,1)S(1)} %pad_maximum_fusion.6), channel_id=1, source_target_pairs={{1,0},{3,2},{5,4},{7,6},{9,8},{11,10},{13,12},{15,14},{17,16},{19,... | collective-permute-start | bytes 19976 | tf_op jit(solution)/shard_map/ppermute | solution.py:24
  153.8 1.7 copy-start.21
  153.8 1.7 %copy-start.32 = (pred[8,9]{0,1:T(8,128)(4,1)S(1)}, pred[8,9]{0,1:T(8,128)(4,1)}, u32[]{:S(2)}) copy-start(pred[8,9]{0,1:T(8,128)(4,1)} %constant.132) | copy-start | bytes 220
  160.7 3.2 %copy-start.13 = (f32[128]{0:T(128)S(1)}, f32[128]{0:T(128)}, u32[]{:S(2)}) copy-start(f32[128]{0:T(128)} %get-tuple-element.15) | copy-start | bytes 1540
  (14 other events, 14.4 us)

commit v2 on v1

--- a/solution.py
+++ b/solution.py
@@ -12,18 +12,7 @@
 PACK = 4
 HALF = 16
 LANES = 4
-
-
-def with_halo(block, sides, before, after):
-    for axis, dim in sides:
-        count = lax.axis_size(axis)
-        forward = [(i, i + 1) for i in range(count - 1)]
-        backward = [(target, source) for source, target in forward]
-        size = block.shape[dim]
-        low = lax.ppermute(lax.slice_in_dim(block, size - before, size, axis=dim), axis, forward)
-        high = lax.ppermute(lax.slice_in_dim(block, 0, after, axis=dim), axis, backward)
-        block = jnp.concatenate([low, block, high], axis=dim)
-    return block
+SIDE = 16
 
 
 def encode_kernel(tiles, x_ref, meta_ref, w1_ref, w2_ref, b1_ref, b2_ref, out_ref):
@@ -136,28 +125,195 @@
     )(cells, vectors)
 
 
-def conv_valid(padded, kernel, bias_vec, stride):
-    summed = lax.conv_general_dilated(
-        padded[None],
-        jnp.swapaxes(kernel, 2, 3),
-        (stride, stride),
-        "VALID",
-        dimension_numbers=("NHWC", "HWIO", "NHWC"),
-        preferred_element_type=jnp.float32,
-    )[0]
-    return jax.nn.relu(summed + bias_vec).astype(jnp.bfloat16)
-
-
-def inside(block, edge):
-    rows, cols, _ = block.shape
-    own = (rows - 2 * edge, cols - 2 * edge)
-    keep = None
-    for dim, axis in enumerate(("row", "col")):
-        place = lax.broadcasted_iota(jnp.int32, (rows, cols, 1), dim) - edge
-        place = place + lax.axis_index(axis) * own[dim]
-        good = (place >= 0) & (place < own[dim] * lax.axis_size(axis))
-        keep = good if keep is None else keep & good
-    return jnp.where(keep, block, jnp.zeros((), block.dtype))
+def around(count_rows, count_cols):
+    return [
+        (dr, dc)
+        for dr in (-1, 0, 1)
+        for dc in (-1, 0, 1)
+        if (dr, dc) != (0, 0) and (dr == 0 or count_rows > 1) and (dc == 0 or count_cols > 1)
+    ]
+
+
+def span_of(step, before, size, after):
+    if step > 0:
+        return slice(size - before, size), slice(0, before)
+    if step < 0:
+        return slice(0, after), slice(before + size, before + size + after)
+    return slice(0, size), slice(before, before + size)
+
+
+def halo_kernel(before, after, x_ref, ext_ref, send_sem, recv_sem):
+    rows, cols, chan = x_ref.shape
+    count_rows, count_cols = lax.axis_size("row"), lax.axis_size("col")
+    my_row, my_col = lax.axis_index("row"), lax.axis_index("col")
+    steps = around(count_rows, count_cols)
+
+    def exists(dr, dc):
+        row, col = my_row + dr, my_col + dc
+        return (row >= 0) & (row < count_rows) & (col >= 0) & (col < count_cols)
+
+    barrier = pltpu.get_barrier_semaphore()
+    for dr, dc in steps:
+
+        @pl.when(exists(dr, dc))
+        def _():
+            pl.semaphore_signal(
+                barrier,
+                inc=1,
+                device_id={"row": my_row + dr, "col": my_col + dc},
+                device_id_type=pl.DeviceIdType.MESH,
+            )
+
+    peers = sum(jnp.where(exists(dr, dc), 1, 0) for dr, dc in steps)
+    pl.semaphore_wait(barrier, peers)
+
+    def copy_of(place):
+        dr, dc = steps[place]
+        row_from, row_to = span_of(dr, before, rows, after)
+        col_from, col_to = span_of(dc, SIDE, cols, SIDE)
+        return pltpu.make_async_remote_copy(
+            src_ref=x_ref.at[row_from, col_from, :],
+            dst_ref=ext_ref.at[row_to, col_to, :],
+            send_sem=send_sem.at[place],
+            recv_sem=recv_sem.at[place],
+            device_id={"row": my_row + dr, "col": my_col + dc},
+            device_id_type=pl.DeviceIdType.MESH,
+        )
+
+    for place, (dr, dc) in enumerate(steps):
+
+        @pl.when(exists(dr, dc))
+        def _():
+            copy_of(place).start()
+
+    ext_ref[before : before + rows, SIDE : SIDE + cols, :] = x_ref[...]
+    for dr in (-1, 0, 1):
+        for dc in (-1, 0, 1):
+            if (dr, dc) == (0, 0):
+                continue
+            row_to = span_of(dr, before, rows, after)[1]
+            col_to = span_of(dc, SIDE, cols, SIDE)[1]
+            shape = (row_to.stop - row_to.start, col_to.stop - col_to.start, chan)
+
+            @pl.when(jnp.logical_not(exists(-dr, -dc)))
+            def _():
+                ext_ref[row_to, col_to, :] = jnp.zeros(shape, ext_ref.dtype)
+
+    for place, (dr, dc) in enumerate(steps):
+
+        @pl.when(exists(dr, dc))
+        def _():
+            copy_of(place).wait_send()
+
+        @pl.when(exists(-dr, -dc))
+        def _():
+            copy_of(place).wait_recv()
+
+
+def with_halo(block, before, after, call_id):
+    rows, cols, chan = block.shape
+    count = len(around(lax.axis_size("row"), lax.axis_size("col")))
+    return pl.pallas_call(
+        functools.partial(halo_kernel, before, after),
+        in_specs=[pl.BlockSpec(memory_space=pltpu.VMEM)],
+        out_specs=pl.BlockSpec(memory_space=pltpu.VMEM),
+        out_shape=jax.ShapeDtypeStruct(
+            (rows + before + after, cols + 2 * SIDE, chan), block.dtype
+        ),
+        scratch_shapes=[
+            pltpu.SemaphoreType.DMA((count,)),
+            pltpu.SemaphoreType.DMA((count,)),
+        ],
+        compiler_params=pltpu.CompilerParams(collective_id=call_id, has_side_effects=True),
+        name=f"halo_{call_id}",
+    )(block)
+
+
+def level_kernel(
+    stride, ext_ref, wa_ref, wb_ref, ba_ref, bb_ref, out_ref, ta, tb, stage_a, cat_a, stage_b, cat_b
+):
+    ext_rows, ext_cols, chan_in = ext_ref.shape
+    rows, cols, chan = out_ref.shape
+    mid_rows, mid_cols, _ = cat_b.shape
+    edge = SIDE // stride
+    for w_ref, t_ref in ((wa_ref, ta), (wb_ref, tb)):
+        deep = w_ref.shape[3]
+        for u in range(3):
+            for v in range(3):
+                flip = w_ref[u, v].astype(jnp.float32).T
+                t_ref[u, v * deep : (v + 1) * deep, :] = flip.astype(jnp.bfloat16)
+    for stage in (stage_a, stage_b):
+        stage[0:8, :] = jnp.zeros((8, stage.shape[1]), jnp.float32)
+        stage[stage.shape[0] - 8 :, :] = jnp.zeros((8, stage.shape[1]), jnp.float32)
+
+    def gather(stage, values, count, step):
+        stage[8 : 8 + values.shape[0], :] = values
+        if step == 1:
+            parts = [stage[7 + v : 7 + v + count, :] for v in range(3)]
+        else:
+            parts = [stage[pl.ds(7 + v, count, stride=step), :] for v in range(3)]
+        return jnp.concatenate(parts, axis=1).astype(jnp.bfloat16)
+
+    def first(r, carry):
+        cat_a[r] = gather(stage_a, ext_ref[r].astype(jnp.float32), mid_cols, stride)
+        return carry
+
+    lax.fori_loop(0, ext_rows, first, 0)
+
+    col = lax.broadcasted_iota(jnp.int32, (mid_cols, chan), 0) - edge
+    col = col + lax.axis_index("col") * cols
+    col_good = (col >= 0) & (col < cols * lax.axis_size("col"))
+    row_base = lax.axis_index("row") * rows
+    row_limit = rows * lax.axis_size("row")
+
+    def second(i, carry):
+        total = jnp.broadcast_to(ba_ref[...], (mid_cols, chan))
+        for u in range(3):
+            total = total + jnp.dot(
+                cat_a[stride * i + u], ta[u], preferred_element_type=jnp.float32
+            )
+        total = jnp.maximum(total, 0.0).astype(jnp.bfloat16).astype(jnp.float32)
+        row = row_base + i - 1
+        total = jnp.where(col_good & (row >= 0) & (row < row_limit), total, 0.0)
+        cat_b[i] = gather(stage_b, total, mid_cols, 1)
+        return carry
+
+    lax.fori_loop(0, mid_rows, second, 0)
+
+    def third(i, carry):
+        total = jnp.broadcast_to(bb_ref[...], (mid_cols, chan))
+        for u in range(3):
+            total = total + jnp.dot(cat_b[i + u], tb[u], preferred_element_type=jnp.float32)
+        total = jnp.maximum(total, 0.0)
+        out_ref[i] = total[edge : edge + cols].astype(jnp.bfloat16)
+        return carry
+
+    lax.fori_loop(0, rows, third, 0)
+
+
+def level(block, kernel_a, kernel_b, bias_a, bias_b, stride, call_id):
+    rows, cols, chan_in = block.shape
+    before, after = (2, 2) if stride == 1 else (3, 2)
+    ext = with_halo(block, before, after, call_id)
+    chan = kernel_a.shape[2]
+    rows_out, cols_out = rows // stride, cols // stride
+    mid_rows, mid_cols = rows_out + 2, ext.shape[1] // stride
+    vmem = pl.BlockSpec(memory_space=pltpu.VMEM)
+    return pl.pallas_call(
+        functools.partial(level_kernel, stride),
+        in_specs=[vmem] * 5,
+        out_specs=vmem,
+        out_shape=jax.ShapeDtypeStruct((rows_out, cols_out, chan), jnp.bfloat16),
+        scratch_shapes=[
+            pltpu.VMEM((3, 3 * chan_in, chan), jnp.bfloat16),
+            pltpu.VMEM((3, 3 * chan, chan), jnp.bfloat16),
+            pltpu.VMEM((ext.shape[1] + 16, chan_in), jnp.float32),
+            pltpu.VMEM((ext.shape[0], mid_cols, 3 * chan_in), jnp.bfloat16),
+            pltpu.VMEM((mid_cols + 16, chan), jnp.float32),
+            pltpu.VMEM((mid_rows, mid_cols, 3 * chan), jnp.bfloat16),
+        ],
+        name=f"level_{call_id}",
+    )(ext, kernel_a, kernel_b, bias_a[None], bias_b[None])
 
 
 def lift_layer(inputs, kernel, bias_vec):
@@ -232,15 +388,9 @@
     place = vectors[:, chan : chan + 2, :].astype(jnp.int32)
     cells = (place[:, 0] * COLS_DEV + place[:, 1]).reshape(-1)
     bev = scatter_max(cells, vectors, chan).reshape(ROWS_DEV, COLS_DEV, chan)
-    sides = (("row", 0), ("col", 1))
-    level_one_a = inside(conv_valid(with_halo(bev, sides, 2, 2), first_conv, pieces[2], 1), 1)
-    level_one = conv_valid(level_one_a, second_conv, pieces[3], 1)
-    level_two_a = inside(conv_valid(with_halo(level_one, sides, 3, 2), third_conv, pieces[4], 2), 1)
-    level_two = conv_valid(level_two_a, fourth_conv, pieces[5], 1)
-    level_three_a = inside(
-        conv_valid(with_halo(level_two, sides, 3, 2), fifth_conv, pieces[6], 2), 1
-    )
-    level_three = conv_valid(level_three_a, sixth_conv, pieces[7], 1)
+    level_one = level(bev, first_conv, second_conv, pieces[2], pieces[3], 1, 0)
+    level_two = level(level_one, third_conv, fourth_conv, pieces[4], pieces[5], 2, 1)
+    level_three = level(level_two, fifth_conv, sixth_conv, pieces[6], pieces[7], 2, 2)
     near = lift_layer(level_one, near_lift, pieces[8])
     middle = lift_layer(level_two, mid_lift, pieces[9])
     distant = lift_layer(level_three, far_lift, pieces[10])

time: 170 us -> 139 us (0.82)
  Pallas kernels: 23.5 us -> 88.3 us
  starting transfers between devices: 39.8 us -> 6.72 us
  local copies, waits for them, and re-layouts: 46.6 us -> 16.8 us
  matrix products: 15.4 us -> 3.85 us
  other arithmetic: 19.3 us -> 8.86 us
  waiting for transfers between devices: 23.5 us -> 13.5 us
    pallas_call x0 -> x6, Pallas kernels: none -> 64.7 us  [the longest x3 33.7 us: with_halo(): pl.pallas_call(functools.partial(halo_kernel, before, after), in_specs=[p...]
    ppermute x12 -> x0, starting transfers between devices: 33.2 us -> none  [the longest x6 22.5 us: with_halo(): lax.ppermute(lax.slice_in_dim(block, 0, after, axis=dim), axis, backward)]
    conv_general_dilated x19 -> x0, local copies, waits for them, and re-layouts: 13.4 us -> none  [conv_valid(): lax.conv_general_dilated(padded[None], jnp.swapaxes(kernel, 2, 3), (strid...]
    conv_general_dilated x6 -> x0, matrix products: 9.39 us -> none  [conv_valid(): lax.conv_general_dilated(padded[None], jnp.swapaxes(kernel, 2, 3), (strid...]
    ppermute x12 -> x0, waiting for transfers between devices: 9.24 us -> none  [the longest x6 7.27 us: with_halo(): lax.ppermute(lax.slice_in_dim(block, 0, after, axis=dim), axis, backward)]
    convert_element_type x10 -> x0, local copies, waits for them, and re-layouts: 4.38 us -> none  [conv_valid(): return jax.nn.relu(summed + bias_vec).astype(jnp.bfloat16)]
    slice x7 -> x0, local copies, waits for them, and re-layouts: 3.54 us -> none  [the longest x4 2.1 us: with_halo(): lax.slice_in_dim(block, size - before, size, axis=dim)]
    unnamed x69 -> x29, local copies, waits for them, and re-layouts: 6.21 us -> 2.77 us
  transfers between devices with their start and end apart: 13 -> 1, of which waited for: 5 -> 1; matrix products, arithmetic and copies ran while one was open for 10% -> 2% of each run, Pallas kernels for 0% -> 0%
where the time goes in v2:
time: 139 us; the launch traced here: 138 us
  Pallas kernels  88.3 us (64%)
  local copies, waits for them, and re-layouts  16.8 us (12%)
  waiting for transfers between devices  13.5 us (10%)
  other arithmetic  8.86 us (6%)
  starting transfers between devices  6.72 us (5%)
  matrix products  3.85 us (3%)
    pallas_call x3, Pallas kernels, with_halo(): pl.pallas_call(functools.partial(halo_kernel, before, after), in_specs=[p...  33.7 us
    pallas_call x3, Pallas kernels, level(): pl.pallas_call(functools.partial(level_kernel, stride), in_specs=[vmem] *...  31 us
    pallas_call x1, Pallas kernels, encode_all(): pl.pallas_call(functools.partial(encode_kernel, step), grid=(tiles // ste...  13.5 us
    all_to_all x1, waiting for transfers between devices, on_device(): lax.all_to_all(encoded, ('row', 'col'), split_axis=0, concat_axis=0, tile...  13.5 us
    pallas_call x1, Pallas kernels, scatter_max(): pl.pallas_call(scatter_kernel, in_specs=[pl.BlockSpec(memory_space=pltpu....  10 us
    all_to_all x1, starting transfers between devices, on_device(): lax.all_to_all(encoded, ('row', 'col'), split_axis=0, concat_axis=0, tile...  6.72 us
    dot_general x3, matrix products, lift_layer(): jnp.einsum('oak,ijk->oiaj', weight, wide, preferred_element_type=jnp.floa...  3.85 us
    concatenate x1, local copies, waits for them, and re-layouts, on_device(): return jnp.concatenate([near, middle, distant], axis=0)  3.44 us
  transfers between devices with their start and end apart: 1, of which 1 were waited for; matrix products, arithmetic and copies ran while one was open for 2% of the time, Pallas kernels for 0%

profile of v2, /device:TPU:9, one launch (start us, length us, event | category | flops | bytes accessed | tf_op | source)
XLA Modules:
  0.0 138.2 jit_solution(970736754682059478)
XLA Ops:
  0.0 0.7 add_select_fusion.1
  0.8 0.7 reshape.175
  1.5 1.5 %slice_bitcast_fusion.2 = (f32[1,64]{1,0:T(1,128)}, f32[1,64]{1,0:T(1,128)}, f32[64,1]{0,1:T(1,128)S(1)}, f32[64]{0:T(128)S(1)}) fusion(f32[1408]{0:T(1024)} %param.31), kind=kLoop, calls=%fused_computation.44 | loop fusion | bytes 2048 | tf_op jit(solution)/shard_map/broadcast_in_dim | solution.py:316
  3.1 0.8 broadcast_in_dim_tile.4.b1_ref
  3.8 0.7 copy.25.b2_ref
  4.5 0.9 broadcast_select_fusion.3
  5.4 0.9 select_n.81.w2_ref
  7.9 0.9 broadcast_select_fusion.2.w1_ref
  8.8 0.7 select_select_fusion.meta_ref
  9.5 13.5 %encode.1 = bf16[16,80,256]{2,1,0:T(8,128)(2,1)} custom-call(bf16[9,32,4096]{2,1,0:T(8,128)(2,1)} %x_ref.1, s32[16,8,256]{2,1,0:T(8,128)} %select_select_fusion.meta_ref, bf16[4,256,144]{2,1,0:T(8,128)(2,1)} %broadcast_select_fusion.2.w1_ref, bf16[256,256]{1,0:T(8,128)(2,1)} %select_n.81.w2_ref, f32[256,1]{1,0:T(8,128)} %broadcast_in_dim_tile.4.b1_ref, ...), custom_call_target="tpu_custom_call" | custom-call | tf_op jit(solution)/shard_map/encode/pallas_call | solution.py:64
  23.1 6.7 %all-to-all-start = ((bf16[16,80,256]{2,1,0:T(8,128)(2,1)}), bf16[16,80,256]{2,1,0:T(8,128)(2,1)S(1)}, u32[]{:S(2)}, u32[]{:S(2)}) async-start(bf16[16,80,256]{2,1,0:T(8,128)(2,1)} %encode.1), calls=%async_computation | async-start | bytes 1310720 | tf_op jit(solution)/shard_map/all_to_all | solution.py:386
  29.8 0.9 copy.27.wa_ref
  30.7 0.7 copy.30
  31.5 0.5 iota_compare_fusion.3
  32.1 0.5 fusion.15
  32.6 0.6 fusion.16
  33.2 13.5 %all-to-all-done.vec_ref = bf16[16,80,256]{2,1,0:T(8,128)(2,1)S(1)} async-done(((bf16[16,80,256]{2,1,0:T(8,128)(2,1)}), bf16[16,80,256]{2,1,0:T(8,128)(2,1)S(1)}, u32[]{:S(2)}, u32[]{:S(2)}) %all-to-all-start) | async-done | bytes 655392 | tf_op jit(solution)/shard_map/all_to_all | solution.py:386
  46.7 0.7 slice_add_fusion
  47.5 10.0 %scatter_max.1 = bf16[4096,64]{1,0:T(8,128)(2,1)} custom-call(s32[4096]{0:T(1024)} %bitcast.71, bf16[16,80,256]{2,1,0:T(8,128)(2,1)} %copy-done.2), custom_call_target="tpu_custom_call" | custom-call | tf_op jit(solution)/shard_map/scatter_max/pallas_call | solution.py:114
  57.6 12.0 %halo_0.1.ext_ref = bf16[20,288,64]{2,1,0:T(8,128)(2,1)} custom-call(bf16[16,256,64]{2,1,0:T(8,128)(2,1)} %bitcast.68), custom_call_target="tpu_custom_call" | custom-call | tf_op jit(solution)/shard_map/halo_0/pallas_call | solution.py:216
  69.5 15.8 %level_0.1.x_ref = bf16[16,256,64]{2,1,0:T(8,128)(2,1)} custom-call(bf16[20,288,64]{2,1,0:T(8,128)(2,1)} %halo_0.1.ext_ref, bf16[3,3,64,64]{3,2,1,0:T(8,128)(2,1)} %wa_ref.3, bf16[3,3,64,64]{3,2,1,0:T(8,128)(2,1)} %wb_ref.3, f32[1,64]{1,0:T(1,128)} %get-tuple-element.15.ba_ref, f32[1,64]{1,0:T(1,128)} %get-tuple-element.14.bb_ref), custom_call_target="tpu_custom_call" | custom-call | tf_op jit(solution)/shard_map/level_0/pallas_call | solution.py:302
  85.3 13.0 %halo_1.1.ext_ref = bf16[21,288,64]{2,1,0:T(8,128)(2,1)} custom-call(bf16[16,256,64]{2,1,0:T(8,128)(2,1)} %level_0.1.x_ref), custom_call_target="tpu_custom_call" | custom-call | tf_op jit(solution)/shard_map/halo_1/pallas_call | solution.py:216
  98.3 9.0 %level_1.1.x_ref = bf16[8,128,128]{2,1,0:T(8,128)(2,1)} custom-call(bf16[21,288,64]{2,1,0:T(8,128)(2,1)} %halo_1.1.ext_ref, bf16[3,3,128,64]{3,2,1,0:T(8,128)(2,1)} %copy.27.wa_ref, bf16[3,3,128,128]{3,2,1,0:T(8,128)(2,1)} %wb_ref.4, f32[1,128]{1,0:T(1,128)} %get-tuple-element.10.ba_ref, f32[1,128]{1,0:T(1,128)} %get-tuple-element.9.bb_ref), custom_call_target="tpu_custom_call" | custom-call | tf_op jit(solution)/shard_map/level_1/pallas_call | solution.py:302
  107.3 8.8 %halo_2.1.ext_ref = bf16[13,160,128]{2,1,0:T(8,128)(2,1)} custom-call(bf16[8,128,128]{2,1,0:T(8,128)(2,1)} %level_1.1.x_ref), custom_call_target="tpu_custom_call" | custom-call | tf_op jit(solution)/shard_map/halo_2/pallas_call | solution.py:216
  116.1 6.2 %level_2.1 = bf16[4,64,256]{2,1,0:T(8,128)(2,1)} custom-call(bf16[13,160,128]{2,1,0:T(8,128)(2,1)} %halo_2.1.ext_ref, bf16[3,3,256,128]{3,2,1,0:T(8,128)(2,1)} %wa_ref.4, bf16[3,3,256,256]{3,2,1,0:T(8,128)(2,1)} %wb_ref.5, f32[1,256]{1,0:T(1,128)} %bitcast.73, f32[1,256]{1,0:T(1,128)} %bitcast.72), custom_call_target="tpu_custom_call" | custom-call | tf_op jit(solution)/shard_map/level_2/pallas_call | solution.py:302
  122.3 1.7 %broadcast_select_fusion = bf16[4,64,4,4,256]{4,3,2,1,0:T(4,128)(2,1)S(1)} fusion(pred[4,4]{1,0:T(4,128)(4,1)S(1)} %iota_compare_fusion.2, bf16[4,64,256]{2,1,0:T(8,128)(2,1)} %level_2.1), kind=kLoop, calls=%fused_computation.12 | loop fusion | flops 1048576 | bytes 2228240 | tf_op jit(solution)/shard_map/jit(_where)/select_n | solution.py:324
  124.0 2.7 %reshape.186 = bf16[4,256,1024,1]{2,1,0,3:T(8,128)(2,1)} reshape(bf16[4,64,4,4,256]{4,3,2,1,0:T(4,128)(2,1)S(1)} %broadcast_select_fusion) | data formatting | bytes 4194304 | tf_op jit(solution)/shard_map/jit(_where)/select_n | solution.py:324
  126.7 1.6 %broadcast_select_fusion.1 = bf16[8,128,2,2,128]{4,3,2,1,0:T(2,128)(2,1)S(1)} fusion(pred[2,2]{1,0:T(4,128)(4,1)} %iota_compare_fusion.3, bf16[8,128,128]{2,1,0:T(8,128)(2,1)S(1)} %copy-done.3), kind=kLoop, calls=%fused_computation.13 | loop fusion | flops 524288 | bytes 1310724 | tf_op jit(solution)/shard_map/jit(_where)/select_n | solution.py:324
  128.4 0.7 reshape.184
  129.1 2.9 %fusion.6 = f32[4,256,128,4]{1,2,3,0:T(8,128)S(1)} fusion(bf16[128,4,1024,1]{0,2,1,3:T(8,128)(2,1)S(1)} %bitcast.69, bf16[4,256,1024,1]{2,1,0,3:T(8,128)(2,1)} %reshape.186), kind=kOutput, calls=%fused_computation.10 | convolution fusion | flops 1073741824 | bytes 5242880 | tf_op jit(solution)/shard_map/oak,ijk->oiaj/dot_general | solution.py:331
  133.2 0.8 copy-done.1
  134.8 3.4 %copy.32 = bf16[384,16,256]{2,1,0:T(8,128)(2,1)} copy(bf16[384,16,256]{2,0,1:T(8,128)(2,1)S(1)} %pad_maximum_fusion) | data formatting | bytes 6291456 | tf_op jit(solution)/shard_map/concatenate | solution.py:397
  (47 shorter events, 3.9 us)
Async XLA Ops:
  0.0 133.2 %copy-start = (bf16[1,1,128,64]{2,3,1,0:T(8,128)(2,1)S(1)}, bf16[1,1,128,64]{2,3,1,0:T(8,128)(2,1)}, u32[]{:S(2)}) copy-start(bf16[1,1,128,64]{2,3,1,0:T(8,128)(2,1)} %param.28) | copy-start | bytes 49156
  0.0 7.5 %copy-start.8 = (bf16[64,9]{0,1:T(8,128)(2,1)S(1)}, bf16[64,9]{0,1:T(8,128)(2,1)}, u32[]{:S(2)}) copy-start(bf16[64,9]{0,1:T(8,128)(2,1)} %param.20) | copy-start | bytes 3460
  0.0 7.8 %copy-start.12 = (s32[16]{0:T(128)S(1)}, s32[16]{0:T(128)}, u32[]{:S(2)}) copy-start(s32[16]{0:T(128)} %param.19) | copy-start | bytes 196
  9.5 20.3 %copy-start.5 = (bf16[3,3,128,64]{2,3,1,0:T(8,128)(2,1)S(1)}, bf16[3,3,128,64]{2,3,1,0:T(8,128)(2,1)}, u32[]{:S(2)}) copy-start(bf16[3,3,128,64]{2,3,1,0:T(8,128)(2,1)} %param.24) | copy-start | bytes 442372
  9.5 21.2 %copy-start.4 = (bf16[4,4,128,256]{3,2,1,0:T(8,128)(2,1)S(1)}, bf16[4,4,128,256]{3,2,1,0:T(8,128)(2,1)}, u32[]{:S(2)}) copy-start(bf16[4,4,128,256]{3,2,1,0:T(8,128)(2,1)} %param.30) | copy-start | bytes 3145732
  23.1 8.3 %copy-start.6 = (bf16[2,2,128,128]{3,2,1,0:T(8,128)(2,1)S(1)}, bf16[2,2,128,128]{3,2,1,0:T(8,128)(2,1)}, u32[]{:S(2)}) copy-start(bf16[2,2,128,128]{3,2,1,0:T(8,128)(2,1)} %param.29) | copy-start | bytes 393220
  23.1 9.0 %copy-start.7 = (f32[1408]{0:T(1024)S(1)}, f32[1408]{0:T(1024)}, u32[]{:S(2)}) copy-start(f32[1408]{0:T(1024)} %param.31) | copy-start | bytes 16900
  23.1 23.6 %all-to-all-start = ((bf16[16,80,256]{2,1,0:T(8,128)(2,1)}), bf16[16,80,256]{2,1,0:T(8,128)(2,1)S(1)}, u32[]{:S(2)}, u32[]{:S(2)}) async-start(bf16[16,80,256]{2,1,0:T(8,128)(2,1)} %encode.1), calls=%async_computation | async-start | bytes 1310720 | tf_op jit(solution)/shard_map/all_to_all | solution.py:386
  46.7 0.9 copy-start.2
  124.0 2.7 %copy-start.3 = (bf16[8,128,128]{2,1,0:T(8,128)(2,1)S(1)}, bf16[8,128,128]{2,1,0:T(8,128)(2,1)}, u32[]{:S(2)}) copy-start(bf16[8,128,128]{2,1,0:T(8,128)(2,1)} %level_1.1.x_ref) | copy-start | bytes 786436
  129.1 2.9 %copy-start.11 = (f32[128]{0:T(128)S(1)}, f32[128]{0:T(128)}, u32[]{:S(2)}) copy-start(f32[128]{0:T(128)} %get-tuple-element.11) | copy-start | bytes 1540
  132.3 0.6 copy-start.10
  132.8 1.2 copy-start.1
  132.8 1.2 copy-start.9

commit v3 on v2

--- a/solution.py
+++ b/solution.py
@@ -13,18 +13,48 @@
 HALF = 16
 LANES = 4
 SIDE = 16
-
-
-def encode_kernel(tiles, x_ref, meta_ref, w1_ref, w2_ref, b1_ref, b2_ref, out_ref):
+TILE = 128
+
+
+def prepare_kernel(embed_ref, mix_ref, bias_ref, w1_ref, w2_ref, b1_ref, b2_ref):
+    mid, feat = embed_ref.shape
+    chan = mix_ref.shape[0]
+    wide = w1_ref.shape[2]
+    lane = lax.broadcasted_iota(jnp.int32, (feat, wide), 1)
+    spread = lane // HALF == lax.broadcasted_iota(jnp.int32, (feat, wide), 0)
+    spread = jnp.where(spread, 1.0, 0.0).astype(jnp.bfloat16)
+    full = jnp.dot(embed_ref[...], spread, preferred_element_type=jnp.float32)
+    point = lax.broadcasted_iota(jnp.int32, (mid, wide), 1) % HALF
+    for q in range(HALF // PACK):
+        for p in range(PACK):
+            part = jnp.where(point == q * PACK + p, full, 0.0)
+            w1_ref[q, p * mid : (p + 1) * mid, :] = part.astype(jnp.bfloat16)
+    w2_ref[...] = jnp.zeros_like(w2_ref)
+    for p in range(PACK):
+        w2_ref[p * chan : (p + 1) * chan, p * mid : (p + 1) * mid] = mix_ref[...]
+    both = mid + chan
+    column = jnp.broadcast_to(bias_ref[...], (both, both)).T[:, 0:1]
+    for p in range(PACK):
+        b1_ref[p * mid : (p + 1) * mid, :] = column[0:mid]
+    b2_ref[...] = column[mid:both]
+
+
+def encode_kernel(x_ref, meta_ref, w1_ref, w2_ref, b1_ref, b2_ref, out_ref, send_ref, ssem, rsem):
+    feat, points, _ = x_ref.shape
+    tiles, _, cap = meta_ref.shape
     chan = b2_ref.shape[0]
-    cap = meta_ref.shape[2]
-    points = x_ref.shape[1]
-    feat = x_ref.shape[0]
-    for t in range(tiles):
-        count = meta_ref[t, 0:1, :]
+    col_count = lax.axis_size("col")
+    me = lax.axis_index("row") * col_count + lax.axis_index("col")
+
+    def device_of(tile):
+        return {"row": tile // col_count, "col": tile % col_count}
+
+    def encode(tile, dest_ref):
+        count = meta_ref[tile, 0:1, :]
+        start = pl.multiple_of(tile * cap, cap)
         best = jnp.full((chan, cap), -jnp.inf, jnp.float32)
         for h in range(points // HALF):
-            block = x_ref[:, h * HALF : (h + 1) * HALF, t * cap : (t + 1) * cap]
+            block = x_ref[:, h * HALF : (h + 1) * HALF, pl.ds(start, cap)]
             block = block.reshape(feat * HALF, cap)
             for q in range(HALF // PACK):
                 hidden = jnp.dot(w1_ref[q], block, preferred_element_type=jnp.float32)
@@ -35,47 +65,84 @@
                     part = second[p * chan : (p + 1) * chan]
                     best = jnp.maximum(best, jnp.where(count > j, part, -jnp.inf))
         vec = jnp.maximum(best + b2_ref[...], 0.0)
-        out_ref[t, 0:chan, :] = vec.astype(jnp.bfloat16)
+        dest_ref[tile, 0:chan, :] = vec.astype(jnp.bfloat16)
         which = lax.broadcasted_iota(jnp.int32, (16, cap), 0)
-        row = jnp.broadcast_to(meta_ref[t, 1:2, :], (16, cap))
-        col = jnp.broadcast_to(meta_ref[t, 2:3, :], (16, cap))
+        row = jnp.broadcast_to(meta_ref[tile, 1:2, :], (16, cap))
+        col = jnp.broadcast_to(meta_ref[tile, 2:3, :], (16, cap))
         tail = jnp.where(which == 0, row, jnp.where(which == 1, col, 0))
-        out_ref[t, chan : chan + 16, :] = tail.astype(jnp.float32).astype(jnp.bfloat16)
-
-
-def encode_all(points, meta, embed, mix, b_embed, b_mix):
-    feat, point_num, slots = points.shape
+        dest_ref[tile, chan : chan + 16, :] = tail.astype(jnp.float32).astype(jnp.bfloat16)
+
+    def copy_of(i, slot):
+        tile = (me + i) % tiles
+        return pltpu.make_async_remote_copy(
+            src_ref=send_ref.at[tile],
+            dst_ref=out_ref.at[slot],
+            send_sem=ssem.at[i],
+            recv_sem=rsem.at[i],
+            device_id=device_of(tile),
+            device_id_type=pl.DeviceIdType.MESH,
+        )
+
+    barrier = pltpu.get_barrier_semaphore()
+
+    def greet(i, carry):
+        pl.semaphore_signal(
+            barrier,
+            inc=1,
+            device_id=device_of((me + i) % tiles),
+            device_id_type=pl.DeviceIdType.MESH,
+        )
+        return carry
+
+    lax.fori_loop(1, tiles, greet, 0)
+    pl.semaphore_wait(barrier, tiles - 1)
+
+    def step(i, carry):
+        encode((me + i) % tiles, send_ref)
+        copy_of(i, me).start()
+        return carry
+
+    lax.fori_loop(1, tiles, step, 0)
+    encode(me, out_ref)
+
+    def finish(i, carry):
+        copy_of(i, me).wait_send()
+        copy_of(i, (me - i + tiles) % tiles).wait_recv()
+        return carry
+
+    lax.fori_loop(1, tiles, finish, 0)
+
+
+def encode_all(points, meta, embed, mix, bias):
+    feat = points.shape[0]
     tiles, _, cap = meta.shape
-    chan = mix.shape[0]
-    mid = embed.shape[0]
-    groups = HALF // PACK
-    pick = (
-        jnp.arange(HALF)[None, None, :]
-        == PACK * jnp.arange(groups)[:, None, None] + jnp.arange(PACK)[None, :, None]
-    )
-    w1 = jnp.where(pick[:, :, None, None, :], embed[None, None, :, :, None], 0)
-    w1 = w1.reshape(groups, PACK * mid, feat * HALF).astype(jnp.bfloat16)
-    eye = jnp.eye(PACK, dtype=jnp.bool_)
-    w2 = jnp.where(eye[:, None, :, None], mix[None, :, None, :], 0)
-    w2 = w2.reshape(PACK * chan, PACK * mid).astype(jnp.bfloat16)
-    b1 = jnp.tile(b_embed, PACK)[:, None]
-    b2 = b_mix[:, None]
-    step = 2
+    mid, chan = embed.shape[0], mix.shape[0]
+    vmem = pl.BlockSpec(memory_space=pltpu.VMEM)
+    weights = pl.pallas_call(
+        prepare_kernel,
+        in_specs=[vmem] * 3,
+        out_specs=[vmem] * 4,
+        out_shape=[
+            jax.ShapeDtypeStruct((HALF // PACK, PACK * mid, feat * HALF), jnp.bfloat16),
+            jax.ShapeDtypeStruct((PACK * chan, PACK * mid), jnp.bfloat16),
+            jax.ShapeDtypeStruct((PACK * mid, 1), jnp.float32),
+            jax.ShapeDtypeStruct((chan, 1), jnp.float32),
+        ],
+        name="prepare",
+    )(embed, mix, bias)
     return pl.pallas_call(
-        functools.partial(encode_kernel, step),
-        grid=(tiles // step,),
-        in_specs=[
-            pl.BlockSpec((feat, point_num, step * cap), lambda i: (0, 0, i)),
-            pl.BlockSpec((step, 8, cap), lambda i: (i, 0, 0)),
-            pl.BlockSpec(w1.shape, lambda i: (0, 0, 0)),
-            pl.BlockSpec(w2.shape, lambda i: (0, 0)),
-            pl.BlockSpec(b1.shape, lambda i: (0, 0)),
-            pl.BlockSpec(b2.shape, lambda i: (0, 0)),
+        encode_kernel,
+        in_specs=[vmem] * 6,
+        out_specs=vmem,
+        out_shape=jax.ShapeDtypeStruct((tiles, chan + 16, cap), jnp.bfloat16),
+        scratch_shapes=[
+            pltpu.VMEM((tiles, chan + 16, cap), jnp.bfloat16),
+            pltpu.SemaphoreType.DMA((tiles,)),
+            pltpu.SemaphoreType.DMA((tiles,)),
         ],
-        out_specs=pl.BlockSpec((step, chan + 16, cap), lambda i: (i, 0, 0)),
-        out_shape=jax.ShapeDtypeStruct((tiles, chan + 16, cap), jnp.bfloat16),
-        name="encode",
-    )(points, meta, w1, w2, b1, b2)
+        compiler_params=pltpu.CompilerParams(collective_id=7, has_side_effects=True),
+        name="encode_send",
+    )(points, meta, *weights)
 
 
 def scatter_kernel(cell_ref, vec_ref, out_ref, stage, *grids):
@@ -230,7 +297,8 @@
 
 
 def level_kernel(
-    stride, ext_ref, wa_ref, wb_ref, ba_ref, bb_ref, out_ref, ta, tb, stage_a, cat_a, stage_b, cat_b
+    stride, factor, ext_ref, wa_ref, wb_ref, ba_ref, bb_ref, out_ref, wide_ref,
+    ta, tb, stage_a, cat_a, stage_b, cat_b, wide
 ):
     ext_rows, ext_cols, chan_in = ext_ref.shape
     rows, cols, chan = out_ref.shape
@@ -246,6 +314,8 @@
         stage[0:8, :] = jnp.zeros((8, stage.shape[1]), jnp.float32)
         stage[stage.shape[0] - 8 :, :] = jnp.zeros((8, stage.shape[1]), jnp.float32)
 
+    wide[...] = jnp.zeros_like(wide)
+
     def gather(stage, values, count, step):
         stage[8 : 8 + values.shape[0], :] = values
         if step == 1:
@@ -258,7 +328,7 @@
         cat_a[r] = gather(stage_a, ext_ref[r].astype(jnp.float32), mid_cols, stride)
         return carry
 
-    lax.fori_loop(0, ext_rows, first, 0)
+    lax.fori_loop(0, ext_rows, first, 0, unroll=2)
 
     col = lax.broadcasted_iota(jnp.int32, (mid_cols, chan), 0) - edge
     col = col + lax.axis_index("col") * cols
@@ -278,20 +348,29 @@
         cat_b[i] = gather(stage_b, total, mid_cols, 1)
         return carry
 
-    lax.fori_loop(0, mid_rows, second, 0)
+    lax.fori_loop(0, mid_rows, second, 0, unroll=2)
 
     def third(i, carry):
         total = jnp.broadcast_to(bb_ref[...], (mid_cols, chan))
         for u in range(3):
             total = total + jnp.dot(cat_b[i + u], tb[u], preferred_element_type=jnp.float32)
         total = jnp.maximum(total, 0.0)
-        out_ref[i] = total[edge : edge + cols].astype(jnp.bfloat16)
+        total = total[edge : edge + cols]
+        out_ref[i] = total.astype(jnp.bfloat16)
+        if factor > 1:
+            parts = chan // TILE
+            for b in range(factor):
+                for k in range(parts):
+                    piece = total[:, k * TILE : (k + 1) * TILE]
+                    wide[b * parts + k, pl.ds(b, cols, stride=factor), :] = piece
+            for k in range(factor * parts):
+                wide_ref[i, :, k * TILE : (k + 1) * TILE] = wide[k].astype(jnp.bfloat16)
         return carry
 
-    lax.fori_loop(0, rows, third, 0)
-
-
-def level(block, kernel_a, kernel_b, bias_a, bias_b, stride, call_id):
+    lax.fori_loop(0, rows, third, 0, unroll=2)
+
+
+def level(block, kernel_a, kernel_b, bias_a, bias_b, stride, factor, call_id):
     rows, cols, chan_in = block.shape
     before, after = (2, 2) if stride == 1 else (3, 2)
     ext = with_halo(block, before, after, call_id)
@@ -299,11 +378,15 @@
     rows_out, cols_out = rows // stride, cols // stride
     mid_rows, mid_cols = rows_out + 2, ext.shape[1] // stride
     vmem = pl.BlockSpec(memory_space=pltpu.VMEM)
+    wide_shape = (rows_out, cols_out * factor, chan * factor) if factor > 1 else (1, 16, 128)
     return pl.pallas_call(
-        functools.partial(level_kernel, stride),
+        functools.partial(level_kernel, stride, factor),
         in_specs=[vmem] * 5,
-        out_specs=vmem,
-        out_shape=jax.ShapeDtypeStruct((rows_out, cols_out, chan), jnp.bfloat16),
+        out_specs=[vmem, vmem],
+        out_shape=[
+            jax.ShapeDtypeStruct((rows_out, cols_out, chan), jnp.bfloat16),
+            jax.ShapeDtypeStruct(wide_shape, jnp.bfloat16),
+        ],
         scratch_shapes=[
             pltpu.VMEM((3, 3 * chan_in, chan), jnp.bfloat16),
             pltpu.VMEM((3, 3 * chan, chan), jnp.bfloat16),
@@ -311,25 +394,18 @@
             pltpu.VMEM((ext.shape[0], mid_cols, 3 * chan_in), jnp.bfloat16),
             pltpu.VMEM((mid_cols + 16, chan), jnp.float32),
             pltpu.VMEM((mid_rows, mid_cols, 3 * chan), jnp.bfloat16),
+            pltpu.VMEM((factor * chan // TILE, cols_out * factor, TILE) if factor > 1 else (1, 8, TILE), jnp.float32),
         ],
         name=f"level_{call_id}",
     )(ext, kernel_a, kernel_b, bias_a[None], bias_b[None])
 
 
-def lift_layer(inputs, kernel, bias_vec):
+def lift_layer(wide, kernel, bias_vec):
     factor = kernel.shape[0]
-    rows, cols, chan = inputs.shape
-    if factor > 1:
-        eye = jnp.eye(factor, dtype=jnp.bool_)
-        wide = jnp.where(
-            eye[None, None, :, :, None], inputs[:, :, None, None, :], jnp.zeros((), inputs.dtype)
-        )
-        wide = wide.reshape(rows, cols * factor, factor * chan)
-    else:
-        wide = inputs
-    weight = jnp.transpose(kernel, (2, 0, 1, 3)).reshape(kernel.shape[2], factor, factor * chan)
+    rows, cols, depth = wide.shape
+    weight = jnp.transpose(kernel, (2, 0, 1, 3)).reshape(kernel.shape[2], factor, depth)
     product = jnp.einsum("oak,ijk->oiaj", weight, wide, preferred_element_type=jnp.float32)
-    product = product.reshape(kernel.shape[2], rows * factor, cols * factor)
+    product = product.reshape(kernel.shape[2], rows * factor, cols)
     return jax.nn.relu(product + bias_vec[:, None, None]).astype(jnp.bfloat16)
 
 
@@ -382,18 +458,22 @@
         live_points[:, None, :],
         jnp.where(which == 1, row_local[:, None, :], col_local[:, None, :]),
     )
-    encoded = encode_all(points, meta, point_embed, point_mix, pieces[0], pieces[1])
-    vectors = lax.all_to_all(encoded, ("row", "col"), split_axis=0, concat_axis=0, tiled=True)
+    lead = biases[: extents[0] + extents[1]].reshape(1, -1)
+    vectors = encode_all(points, meta, point_embed, point_mix, lead)
     chan = point_mix.shape[0]
     place = vectors[:, chan : chan + 2, :].astype(jnp.int32)
     cells = (place[:, 0] * COLS_DEV + place[:, 1]).reshape(-1)
     bev = scatter_max(cells, vectors, chan).reshape(ROWS_DEV, COLS_DEV, chan)
-    level_one = level(bev, first_conv, second_conv, pieces[2], pieces[3], 1, 0)
-    level_two = level(level_one, third_conv, fourth_conv, pieces[4], pieces[5], 2, 1)
-    level_three = level(level_two, fifth_conv, sixth_conv, pieces[6], pieces[7], 2, 2)
+    level_one, _ = level(bev, first_conv, second_conv, pieces[2], pieces[3], 1, 1, 0)
+    level_two, wide_two = level(
+        level_one, third_conv, fourth_conv, pieces[4], pieces[5], 2, mid_lift.shape[0], 1
+    )
+    _, wide_three = level(
+        level_two, fifth_conv, sixth_conv, pieces[6], pieces[7], 2, far_lift.shape[0], 2
+    )
     near = lift_layer(level_one, near_lift, pieces[8])
-    middle = lift_layer(level_two, mid_lift, pieces[9])
-    distant = lift_layer(level_three, far_lift, pieces[10])
+    middle = lift_layer(wide_two, mid_lift, pieces[9])
+    distant = lift_layer(wide_three, far_lift, pieces[10])
     return jnp.concatenate([near, middle, distant], axis=0)
 
 

time: 139 us -> 124 us (0.89)
  waiting for transfers between devices: 13.5 us -> 0 us
  Pallas kernels: 88.3 us -> 97 us
  starting transfers between devices: 6.72 us -> 0 us
  other arithmetic: 8.86 us -> 4.57 us
  matrix products: 3.85 us -> 6.33 us
  local copies, waits for them, and re-layouts: 16.8 us -> 14.8 us
    all_to_all x1 -> x0, waiting for transfers between devices: 13.5 us -> none  [on_device(): lax.all_to_all(encoded, ('row', 'col'), split_axis=0, concat_axis=0, tile...]
    pallas_call x4 -> x5, Pallas kernels: 44.5 us -> 51.4 us  [the longest x3 25.6 us: level(): pl.pallas_call(functools.partial(level_kernel, stride, factor), in_specs=...]
    all_to_all x1 -> x0, starting transfers between devices: 6.72 us -> none  [on_device(): lax.all_to_all(encoded, ('row', 'col'), split_axis=0, concat_axis=0, tile...]
    select_n x4 -> x0, other arithmetic: 5.08 us -> none  [the longest x2 3.36 us: lift_layer(): jnp.where(eye[None, None, :, :, None], inputs[:, :, None, None, :], jnp.z...]
    select_n x3 -> x0, local copies, waits for them, and re-layouts: 4.28 us -> none  [the longest x2 3.41 us: lift_layer(): jnp.where(eye[None, None, :, :, None], inputs[:, :, None, None, :], jnp.z...]
    unnamed x29 -> x10, local copies, waits for them, and re-layouts: 2.77 us -> 6.42 us
    dot_general x3, matrix products: 3.85 us -> 6.33 us  [lift_layer(): jnp.einsum('oak,ijk->oiaj', weight, wide, preferred_element_type=jnp.floa...]
    broadcast_in_dim x7 -> x0, local copies, waits for them, and re-layouts: 2.13 us -> none  [the longest x6 1.44 us: encode_all(): w1 = jnp.where(pick[:, :, None, None, :], embed[None, None, :, :, None], 0)]
  transfers between devices with their start and end apart: 1 -> 0, of which waited for: 1 -> 0; matrix products, arithmetic and copies ran while one was open for 2% -> 0% of each run, Pallas kernels for 0% -> 0%
where the time goes in v3:
time: 124 us; the launch traced here: 123 us
  Pallas kernels  97 us (78%)
  local copies, waits for them, and re-layouts  14.8 us (12%)
  matrix products  6.33 us (5%)
  other arithmetic  4.57 us (4%)
    pallas_call x3, Pallas kernels, with_halo(): pl.pallas_call(functools.partial(halo_kernel, before, after), in_specs=[p...  35.5 us
    pallas_call x3, Pallas kernels, level(): pl.pallas_call(functools.partial(level_kernel, stride, factor), in_specs=...  25.6 us
    pallas_call x1, Pallas kernels, encode_all(): pl.pallas_call(encode_kernel, in_specs=[vmem] * 6, out_specs=vmem, out_sh...  24.1 us
    pallas_call x1, Pallas kernels, scatter_max(): pl.pallas_call(scatter_kernel, in_specs=[pl.BlockSpec(memory_space=pltpu....  10 us
    unnamed x10, local copies, waits for them, and re-layouts  6.42 us
    dot_general x3, matrix products, lift_layer(): jnp.einsum('oak,ijk->oiaj', weight, wide, preferred_element_type=jnp.floa...  6.33 us
    concatenate x1, local copies, waits for them, and re-layouts, on_device(): return jnp.concatenate([near, middle, distant], axis=0)  3.44 us
    slice x2, local copies, waits for them, and re-layouts, on_device(): pieces.append(biases[offset:offset + extent])  2.78 us

profile of v3, /device:TPU:9, one launch (start us, length us, event | category | flops | bytes accessed | tf_op | source)
XLA Modules:
  0.0 122.8 jit_solution(2096201153375685101)
XLA Ops:
  0.0 0.0 copy-start
  0.0 1.4 %slice_bitcast_fusion.2 = (f32[1,64]{1,0:T(1,128)}, f32[1,64]{1,0:T(1,128)}) fusion(f32[1408]{0:T(1024)} %param.31), kind=kLoop, calls=%fused_computation.36 | loop fusion | bytes 1024 | tf_op jit(solution)/shard_map/broadcast_in_dim | solution.py:400
  1.4 1.4 %fusion.16 = (f32[256]{0:T(256)}, f32[256]{0:T(256)}) fusion(f32[1408]{0:T(1024)} %param.31), kind=kLoop, calls=%fused_computation.42 | loop fusion | bytes 4096 | tf_op jit(solution)/shard_map/slice | solution.py:446
  2.8 1.4 %fusion.15 = (f32[128]{0:T(128)S(1)}, f32[128]{0:T(128)S(1)}, f32[1,128]{1,0:T(1,128)}, f32[1,128]{1,0:T(1,128)}, f32[1,128]{1,0:T(1,128)}, /*index=5*/f32[128]{0:T(128)S(1)}) fusion(f32[1408]{0:T(1024)} %param.31), kind=kLoop, calls=%fused_computation.41 | loop fusion | bytes 6144 | tf_op jit(solution)/shard_map/slice | solution.py:446
  4.2 0.7 reshape.70
  4.9 0.7 fusion.13
  5.6 1.4 %copy.21.embed_ref = bf16[64,9]{1,0:T(8,128)(2,1)} copy(bf16[64,9]{0,1:T(8,128)(2,1)} %param.20) | data formatting | bytes 2304 | tf_op args[4]
  7.0 0.7 add_select_fusion.1
  7.8 0.7 select_select_fusion.meta_ref
  8.5 1.0 copy.24
  9.6 1.8 %copy.23.wa_ref = bf16[3,3,128,64]{3,2,1,0:T(8,128)(2,1)} copy(bf16[3,3,128,64]{2,3,1,0:T(8,128)(2,1)} %param.24) | data formatting | bytes 294912 | tf_op args[8]
  11.4 1.8 %prepare.1 = (bf16[4,256,144]{2,1,0:T(8,128)(2,1)}, bf16[256,256]{1,0:T(8,128)(2,1)}, f32[256,1]{1,0:T(8,128)}, f32[64,1]{1,0:T(8,128)}) custom-call(bf16[64,9]{1,0:T(8,128)(2,1)} %copy.21.embed_ref, bf16[64,64]{1,0:T(8,128)(2,1)} %mix_ref.1, f32[1,128]{1,0:T(1,128)} %get-tuple-element.27.bias_ref), custom_call_target="tpu_custom_call" | custom-call | tf_op jit(solution)/shard_map/prepare/pallas_call | solution.py:121
  13.1 24.1 %encode_send.1.vec_ref = bf16[16,80,256]{2,1,0:T(8,128)(2,1)} custom-call(bf16[9,32,4096]{2,1,0:T(8,128)(2,1)} %x_ref.1, s32[16,8,256]{2,1,0:T(8,128)} %select_select_fusion.meta_ref, bf16[4,256,144]{2,1,0:T(8,128)(2,1)} %get-tuple-element.13.w1_ref, bf16[256,256]{1,0:T(8,128)(2,1)} %get-tuple-element.14.w2_ref, f32[256,1]{1,0:T(8,128)} %get-tuple-element.15.b1_ref, ...), custom_call_target="tpu_custom_call" | custom-call | tf_op jit(solution)/shard_map/encode_send/pallas_call | solution.py:133
  37.2 0.9 slice_convert_fusion
  38.1 0.6 slice_add_fusion
  38.7 10.0 %scatter_max.1 = bf16[4096,64]{1,0:T(8,128)(2,1)} custom-call(s32[4096]{0:T(1024)} %bitcast.71, bf16[16,80,256]{2,1,0:T(8,128)(2,1)} %encode_send.1.vec_ref), custom_call_target="tpu_custom_call" | custom-call | tf_op jit(solution)/shard_map/scatter_max/pallas_call | solution.py:181
  48.7 12.1 %halo_0.1.ext_ref = bf16[20,288,64]{2,1,0:T(8,128)(2,1)} custom-call(bf16[16,256,64]{2,1,0:T(8,128)(2,1)} %bitcast.68), custom_call_target="tpu_custom_call" | custom-call | tf_op jit(solution)/shard_map/halo_0/pallas_call | solution.py:283
  60.8 11.6 %level_0.1 = (bf16[16,256,64]{2,1,0:T(8,128)(2,1)}, bf16[1,16,128]{2,1,0:T(8,128)(2,1)}) custom-call(bf16[20,288,64]{2,1,0:T(8,128)(2,1)} %halo_0.1.ext_ref, bf16[3,3,64,64]{3,2,1,0:T(8,128)(2,1)} %wa_ref.3, bf16[3,3,64,64]{3,2,1,0:T(8,128)(2,1)} %wb_ref.3, f32[1,64]{1,0:T(1,128)} %get-tuple-element.32.ba_ref, f32[1,64]{1,0:T(1,128)} %get-tuple-element.31.bb_ref), custom_call_target="tpu_custom_call" | custom-call | tf_op jit(solution)/shard_map/level_0/pallas_call | solution.py:382
  72.5 1.7 %fusion.7 = bf16[128,16,256]{2,0,1:T(8,128)(2,1)S(1)} fusion(bf16[16,256,64]{2,1,0:T(8,128)(2,1)} %get-tuple-element.17.x_ref, f32[128]{0:T(128)S(1)} %get-tuple-element.23, bf16[1,1,128,64]{2,3,1,0:T(8,128)(2,1)S(1)} %copy-done), kind=kOutput, calls=%fused_computation.11 | convolution fusion | flops 68681728 | bytes 1589760 | tf_op jit(solution)/shard_map/oak,ijk->oiaj/dot_general | solution.py:407
  74.2 13.8 %halo_1.1.ext_ref = bf16[21,288,64]{2,1,0:T(8,128)(2,1)} custom-call(bf16[16,256,64]{2,1,0:T(8,128)(2,1)} %get-tuple-element.17.x_ref), custom_call_target="tpu_custom_call" | custom-call | tf_op jit(solution)/shard_map/halo_1/pallas_call | solution.py:283
  88.0 7.2 %level_1.1 = (bf16[8,128,128]{2,1,0:T(8,128)(2,1)}, bf16[8,256,256]{2,1,0:T(8,128)(2,1)}) custom-call(bf16[21,288,64]{2,1,0:T(8,128)(2,1)} %halo_1.1.ext_ref, bf16[3,3,128,64]{3,2,1,0:T(8,128)(2,1)} %copy.23.wa_ref, bf16[3,3,128,128]{3,2,1,0:T(8,128)(2,1)} %wb_ref.4, f32[1,128]{1,0:T(1,128)} %get-tuple-element.26.ba_ref, f32[1,128]{1,0:T(1,128)} %get-tuple-element.25.bb_ref), custom_call_target="tpu_custom_call" | custom-call | tf_op jit(solution)/shard_map/level_1/pallas_call | solution.py:382
  95.2 9.6 %halo_2.1.ext_ref = bf16[13,160,128]{2,1,0:T(8,128)(2,1)} custom-call(bf16[8,128,128]{2,1,0:T(8,128)(2,1)} %get-tuple-element.19.x_ref), custom_call_target="tpu_custom_call" | custom-call | tf_op jit(solution)/shard_map/halo_2/pallas_call | solution.py:283
  104.8 1.7 %fusion.8 = f32[8,256,128,2]{1,2,3,0:T(8,128)S(1)} fusion(bf16[128,2,256,1]{0,2,1,3:T(8,128)(2,1)S(1)} %bitcast.70, bf16[8,256,256]{2,1,0:T(8,128)(2,1)} %get-tuple-element.18), kind=kOutput, calls=%fused_computation.12 | convolution fusion | flops 268435456 | bytes 3276800 | tf_op jit(solution)/shard_map/oak,ijk->oiaj/dot_general | solution.py:407
  106.5 0.0 copy-start.1
  106.5 0.3 fusion.5
  106.9 0.9 copy-done.1
  107.8 1.3 %copy.26 = bf16[4,4,128,256]{2,3,1,0:T(8,128)(2,1)} copy(bf16[4,4,128,256]{3,2,1,0:T(8,128)(2,1)S(1)} %copy-done.1) | data formatting | bytes 2097152 | tf_op args[14]
  109.1 6.8 %level_2.1 = (bf16[4,64,256]{2,1,0:T(8,128)(2,1)}, bf16[4,256,1024]{2,1,0:T(8,128)(2,1)}) custom-call(bf16[13,160,128]{2,1,0:T(8,128)(2,1)} %halo_2.1.ext_ref, bf16[3,3,256,128]{3,2,1,0:T(8,128)(2,1)} %wa_ref.4, bf16[3,3,256,256]{3,2,1,0:T(8,128)(2,1)} %wb_ref.5, f32[1,256]{1,0:T(1,128)} %bitcast.73, f32[1,256]{1,0:T(1,128)} %bitcast.72), custom_call_target="tpu_custom_call" | custom-call | tf_op jit(solution)/shard_map/level_2/pallas_call | solution.py:382
  115.8 2.9 %fusion.2 = f32[4,256,128,4]{1,2,3,0:T(8,128)S(1)} fusion(bf16[128,4,1024,1]{0,2,1,3:T(8,128)(2,1)S(1)} %bitcast.69, bf16[4,256,1024]{2,1,0:T(8,128)(2,1)} %get-tuple-element.20), kind=kOutput, calls=%fused_computation.4 | convolution fusion | flops 1073741824 | bytes 5242880 | tf_op jit(solution)/shard_map/oak,ijk->oiaj/dot_general | solution.py:407
  118.7 0.3 fusion.1
  119.1 0.3 pad_maximum_fusion
  119.3 3.4 %copy.28 = bf16[384,16,256]{2,1,0:T(8,128)(2,1)} copy(bf16[384,16,256]{2,0,1:T(8,128)(2,1)S(1)} %pad_maximum_fusion) | data formatting | bytes 6291456 | tf_op jit(solution)/shard_map/concatenate | solution.py:477
  (6 shorter events, 0.0 us)
Async XLA Ops:
  0.0 72.5 %copy-start = (bf16[1,1,128,64]{2,3,1,0:T(8,128)(2,1)S(1)}, bf16[1,1,128,64]{2,3,1,0:T(8,128)(2,1)}, u32[]{:S(2)}) copy-start(bf16[1,1,128,64]{2,3,1,0:T(8,128)(2,1)} %param.28) | copy-start | bytes 49156
  106.5 1.2 %copy-start.1 = (bf16[4,4,128,256]{3,2,1,0:T(8,128)(2,1)S(1)}, bf16[4,4,128,256]{3,2,1,0:T(8,128)(2,1)}, u32[]{:S(2)}) copy-start(bf16[4,4,128,256]{3,2,1,0:T(8,128)(2,1)} %param.30) | copy-start | bytes 3145732
  109.1 6.8 %copy-start.2 = (bf16[4,4,128,256]{2,3,1,0:T(8,128)(2,1)S(1)}, bf16[4,4,128,256]{2,3,1,0:T(8,128)(2,1)}, u32[]{:S(2)}) copy-start(bf16[4,4,128,256]{2,3,1,0:T(8,128)(2,1)} %copy.26) | copy-start | bytes 3145732

commit v4 on v3

--- a/solution.py
+++ b/solution.py
@@ -33,16 +33,20 @@
     for p in range(PACK):
         w2_ref[p * chan : (p + 1) * chan, p * mid : (p + 1) * mid] = mix_ref[...]
     both = mid + chan
-    column = jnp.broadcast_to(bias_ref[...], (both, both)).T[:, 0:1]
+    column = jnp.broadcast_to(bias_ref[:, 0:both], (both, both)).T[:, 0:1]
     for p in range(PACK):
         b1_ref[p * mid : (p + 1) * mid, :] = column[0:mid]
     b2_ref[...] = column[mid:both]
 
 
-def encode_kernel(x_ref, meta_ref, w1_ref, w2_ref, b1_ref, b2_ref, out_ref, send_ref, ssem, rsem):
+def encode_kernel(
+    x_ref, count_ref, cell_ref, w1_ref, w2_ref, b1_ref, b2_ref, out_ref, place_ref,
+    send_ref, ssem, rsem, place_ssem, place_rsem
+):
     feat, points, _ = x_ref.shape
-    tiles, _, cap = meta_ref.shape
+    tiles, _, cap = count_ref.shape
     chan = b2_ref.shape[0]
+    half = tiles // 2
     col_count = lax.axis_size("col")
     me = lax.axis_index("row") * col_count + lax.axis_index("col")
 
@@ -50,7 +54,7 @@
         return {"row": tile // col_count, "col": tile % col_count}
 
     def encode(tile, dest_ref):
-        count = meta_ref[tile, 0:1, :]
+        count = count_ref[tile]
         start = pl.multiple_of(tile * cap, cap)
         best = jnp.full((chan, cap), -jnp.inf, jnp.float32)
         for h in range(points // HALF):
@@ -65,12 +69,18 @@
                     part = second[p * chan : (p + 1) * chan]
                     best = jnp.maximum(best, jnp.where(count > j, part, -jnp.inf))
         vec = jnp.maximum(best + b2_ref[...], 0.0)
-        dest_ref[tile, 0:chan, :] = vec.astype(jnp.bfloat16)
-        which = lax.broadcasted_iota(jnp.int32, (16, cap), 0)
-        row = jnp.broadcast_to(meta_ref[tile, 1:2, :], (16, cap))
-        col = jnp.broadcast_to(meta_ref[tile, 2:3, :], (16, cap))
-        tail = jnp.where(which == 0, row, jnp.where(which == 1, col, 0))
-        dest_ref[tile, chan : chan + 16, :] = tail.astype(jnp.float32).astype(jnp.bfloat16)
+        dest_ref[tile] = vec.astype(jnp.bfloat16)
+
+    def place_of(i, slot):
+        tile = (me + i) % tiles
+        return pltpu.make_async_remote_copy(
+            src_ref=cell_ref.at[tile],
+            dst_ref=place_ref.at[slot],
+            send_sem=place_ssem.at[i],
+            recv_sem=place_rsem.at[i],
+            device_id=device_of(tile),
+            device_id_type=pl.DeviceIdType.MESH,
+        )
 
     def copy_of(i, slot):
         tile = (me + i) % tiles
@@ -97,25 +107,30 @@
     lax.fori_loop(1, tiles, greet, 0)
     pl.semaphore_wait(barrier, tiles - 1)
 
-    def step(i, carry):
+    def step(k, carry):
+        i = half + (1 - 2 * (k % 2)) * ((k + 1) // 2)
         encode((me + i) % tiles, send_ref)
         copy_of(i, me).start()
+        place_of(i, me).start()
         return carry
 
-    lax.fori_loop(1, tiles, step, 0)
+    lax.fori_loop(0, tiles - 1, step, 0)
     encode(me, out_ref)
+    place_ref[me] = cell_ref[me]
 
     def finish(i, carry):
         copy_of(i, me).wait_send()
+        place_of(i, me).wait_send()
         copy_of(i, (me - i + tiles) % tiles).wait_recv()
+        place_of(i, (me - i + tiles) % tiles).wait_recv()
         return carry
 
     lax.fori_loop(1, tiles, finish, 0)
 
 
-def encode_all(points, meta, embed, mix, bias):
+def encode_all(points, counts, cells, embed, mix, bias):
     feat = points.shape[0]
-    tiles, _, cap = meta.shape
+    tiles, _, cap = counts.shape
     mid, chan = embed.shape[0], mix.shape[0]
     vmem = pl.BlockSpec(memory_space=pltpu.VMEM)
     weights = pl.pallas_call(
@@ -132,17 +147,22 @@
     )(embed, mix, bias)
     return pl.pallas_call(
         encode_kernel,
-        in_specs=[vmem] * 6,
-        out_specs=vmem,
-        out_shape=jax.ShapeDtypeStruct((tiles, chan + 16, cap), jnp.bfloat16),
+        in_specs=[vmem] * 7,
+        out_specs=[vmem, vmem],
+        out_shape=[
+            jax.ShapeDtypeStruct((tiles, chan, cap), jnp.bfloat16),
+            jax.ShapeDtypeStruct((tiles, 1, cap), jnp.int32),
+        ],
         scratch_shapes=[
-            pltpu.VMEM((tiles, chan + 16, cap), jnp.bfloat16),
+            pltpu.VMEM((tiles, chan, cap), jnp.bfloat16),
+            pltpu.SemaphoreType.DMA((tiles,)),
+            pltpu.SemaphoreType.DMA((tiles,)),
             pltpu.SemaphoreType.DMA((tiles,)),
             pltpu.SemaphoreType.DMA((tiles,)),
         ],
         compiler_params=pltpu.CompilerParams(collective_id=7, has_side_effects=True),
         name="encode_send",
-    )(points, meta, *weights)
+    )(points, counts, cells, *weights)
 
 
 def scatter_kernel(cell_ref, vec_ref, out_ref, stage, *grids):
@@ -209,8 +229,16 @@
     return slice(0, size), slice(before, before + size)
 
 
-def halo_kernel(before, after, x_ref, ext_ref, send_sem, recv_sem):
+def halo_kernel(before, after, x_ref, ext_ref, send_sem, recv_sem, *packs):
     rows, cols, chan = x_ref.shape
+    part = cols // 2
+    packed = {}
+    if packs:
+        packed = {(1, 0): packs[0:2], (-1, 0): packs[2:4]}
+        for (dr, dc), (source, _) in packed.items():
+            row_from = span_of(dr, before, rows, after)[0]
+            source[:, :, 0:chan] = x_ref[row_from, 0:part, :]
+            source[:, :, chan : 2 * chan] = x_ref[row_from, part:cols, :]
     count_rows, count_cols = lax.axis_size("row"), lax.axis_size("col")
     my_row, my_col = lax.axis_index("row"), lax.axis_index("col")
     steps = around(count_rows, count_cols)
@@ -238,9 +266,12 @@
         dr, dc = steps[place]
         row_from, row_to = span_of(dr, before, rows, after)
         col_from, col_to = span_of(dc, SIDE, cols, SIDE)
+        source, target = x_ref.at[row_from, col_from, :], ext_ref.at[row_to, col_to, :]
+        if (dr, dc) in packed:
+            source, target = packed[(dr, dc)]
         return pltpu.make_async_remote_copy(
-            src_ref=x_ref.at[row_from, col_from, :],
-            dst_ref=ext_ref.at[row_to, col_to, :],
+            src_ref=source,
+            dst_ref=target,
             send_sem=send_sem.at[place],
             recv_sem=recv_sem.at[place],
             device_id={"row": my_row + dr, "col": my_col + dc},
@@ -275,11 +306,20 @@
         @pl.when(exists(-dr, -dc))
         def _():
             copy_of(place).wait_recv()
+            if (dr, dc) in packed:
+                target = packed[(dr, dc)][1]
+                row_to = span_of(dr, before, rows, after)[1]
+                ext_ref[row_to, SIDE : SIDE + part, :] = target[:, :, 0:chan]
+                ext_ref[row_to, SIDE + part : SIDE + cols, :] = target[:, :, chan : 2 * chan]
 
 
 def with_halo(block, before, after, call_id):
     rows, cols, chan = block.shape
     count = len(around(lax.axis_size("row"), lax.axis_size("col")))
+    packs = []
+    if 2 * chan == TILE and lax.axis_size("row") > 1:
+        for depth in (before, before, after, after):
+            packs.append(pltpu.VMEM((depth, cols // 2, TILE), block.dtype))
     return pl.pallas_call(
         functools.partial(halo_kernel, before, after),
         in_specs=[pl.BlockSpec(memory_space=pltpu.VMEM)],
@@ -290,14 +330,15 @@
         scratch_shapes=[
             pltpu.SemaphoreType.DMA((count,)),
             pltpu.SemaphoreType.DMA((count,)),
-        ],
+        ]
+        + packs,
         compiler_params=pltpu.CompilerParams(collective_id=call_id, has_side_effects=True),
         name=f"halo_{call_id}",
     )(block)
 
 
 def level_kernel(
-    stride, factor, ext_ref, wa_ref, wb_ref, ba_ref, bb_ref, out_ref, wide_ref,
+    stride, factor, bias_at, ext_ref, wa_ref, wb_ref, bias_ref, out_ref, wide_ref,
     ta, tb, stage_a, cat_a, stage_b, cat_b, wide
 ):
     ext_rows, ext_cols, chan_in = ext_ref.shape
@@ -337,7 +378,7 @@
     row_limit = rows * lax.axis_size("row")
 
     def second(i, carry):
-        total = jnp.broadcast_to(ba_ref[...], (mid_cols, chan))
+        total = jnp.broadcast_to(bias_ref[:, bias_at : bias_at + chan], (mid_cols, chan))
         for u in range(3):
             total = total + jnp.dot(
                 cat_a[stride * i + u], ta[u], preferred_element_type=jnp.float32
@@ -351,7 +392,9 @@
     lax.fori_loop(0, mid_rows, second, 0, unroll=2)
 
     def third(i, carry):
-        total = jnp.broadcast_to(bb_ref[...], (mid_cols, chan))
+        total = jnp.broadcast_to(
+            bias_ref[:, bias_at + chan : bias_at + 2 * chan], (mid_cols, chan)
+        )
         for u in range(3):
             total = total + jnp.dot(cat_b[i + u], tb[u], preferred_element_type=jnp.float32)
         total = jnp.maximum(total, 0.0)
@@ -370,7 +413,7 @@
     lax.fori_loop(0, rows, third, 0, unroll=2)
 
 
-def level(block, kernel_a, kernel_b, bias_a, bias_b, stride, factor, call_id):
+def level(block, kernel_a, kernel_b, bias, bias_at, stride, factor, call_id):
     rows, cols, chan_in = block.shape
     before, after = (2, 2) if stride == 1 else (3, 2)
     ext = with_halo(block, before, after, call_id)
@@ -380,8 +423,8 @@
     vmem = pl.BlockSpec(memory_space=pltpu.VMEM)
     wide_shape = (rows_out, cols_out * factor, chan * factor) if factor > 1 else (1, 16, 128)
     return pl.pallas_call(
-        functools.partial(level_kernel, stride, factor),
-        in_specs=[vmem] * 5,
+        functools.partial(level_kernel, stride, factor, bias_at),
+        in_specs=[vmem] * 4,
         out_specs=[vmem, vmem],
         out_shape=[
             jax.ShapeDtypeStruct((rows_out, cols_out, chan), jnp.bfloat16),
@@ -397,7 +440,7 @@
             pltpu.VMEM((factor * chan // TILE, cols_out * factor, TILE) if factor > 1 else (1, 8, TILE), jnp.float32),
         ],
         name=f"level_{call_id}",
-    )(ext, kernel_a, kernel_b, bias_a[None], bias_b[None])
+    )(ext, kernel_a, kernel_b, bias)
 
 
 def lift_layer(wide, kernel, bias_vec):
@@ -450,26 +493,26 @@
     ncols_all = COLS_DEV * lax.axis_size("col")
     live_slot = lax.broadcasted_iota(jnp.int32, (tile_num, capacity), 1) < tile_count[:, None]
     live_points = jnp.where(live_slot, point_count.reshape(tile_num, capacity), 0)
-    row_local = (pillar_cell // ncols_all % ROWS_DEV).reshape(tile_num, capacity)
-    col_local = (pillar_cell % COLS_DEV).reshape(tile_num, capacity)
-    which = lax.broadcasted_iota(jnp.int32, (1, 8, 1), 1)
-    meta = jnp.where(
-        which == 0,
-        live_points[:, None, :],
-        jnp.where(which == 1, row_local[:, None, :], col_local[:, None, :]),
+    row_local = pillar_cell // ncols_all % ROWS_DEV
+    local_cell = row_local * COLS_DEV + pillar_cell % COLS_DEV
+    lead = biases.reshape(1, -1)
+    vectors, places = encode_all(
+        points,
+        live_points.reshape(tile_num, 1, capacity),
+        local_cell.reshape(tile_num, 1, capacity),
+        point_embed,
+        point_mix,
+        lead,
     )
-    lead = biases[: extents[0] + extents[1]].reshape(1, -1)
-    vectors = encode_all(points, meta, point_embed, point_mix, lead)
     chan = point_mix.shape[0]
-    place = vectors[:, chan : chan + 2, :].astype(jnp.int32)
-    cells = (place[:, 0] * COLS_DEV + place[:, 1]).reshape(-1)
+    cells = places.reshape(-1)
     bev = scatter_max(cells, vectors, chan).reshape(ROWS_DEV, COLS_DEV, chan)
-    level_one, _ = level(bev, first_conv, second_conv, pieces[2], pieces[3], 1, 1, 0)
+    level_one, _ = level(bev, first_conv, second_conv, lead, sum(extents[:2]), 1, 1, 0)
     level_two, wide_two = level(
-        level_one, third_conv, fourth_conv, pieces[4], pieces[5], 2, mid_lift.shape[0], 1
+        level_one, third_conv, fourth_conv, lead, sum(extents[:4]), 2, mid_lift.shape[0], 1
     )
     _, wide_three = level(
-        level_two, fifth_conv, sixth_conv, pieces[6], pieces[7], 2, far_lift.shape[0], 2
+        level_two, fifth_conv, sixth_conv, lead, sum(extents[:6]), 2, far_lift.shape[0], 2
     )
     near = lift_layer(level_one, near_lift, pieces[8])
     middle = lift_layer(wide_two, mid_lift, pieces[9])

time: 124 us -> 108 us (0.87)
  Pallas kernels: 97 us -> 89.8 us
  local copies, waits for them, and re-layouts: 14.8 us -> 9.85 us
  matrix products: 6.33 us -> 4.21 us
    pallas_call x3, Pallas kernels: 35.5 us -> 28.3 us  [with_halo(): pl.pallas_call(functools.partial(halo_kernel, before, after), in_specs=[p...]
    dot_general x3, matrix products: 6.33 us -> 4.21 us  [lift_layer(): jnp.einsum('oak,ijk->oiaj', weight, wide, preferred_element_type=jnp.floa...]
    unnamed x10 -> x16, local copies, waits for them, and re-layouts: 6.42 us -> 4.31 us
    slice x2 -> x1, local copies, waits for them, and re-layouts: 2.78 us -> 0.81 us  [on_device(): pieces.append(biases[offset:offset + extent])]
    select_n x2 -> x0, other arithmetic: 1.47 us -> none  [the longest x1 0.74 us: on_device(): pillar_cell // ncols_all % ROWS_DEV]
    broadcast_in_dim x3 -> x0, local copies, waits for them, and re-layouts: 1.42 us -> none  [the longest x1 1.41 us: level(): bias_b[None]]
where the time goes in v4:
time: 108 us
  Pallas kernels  89.8 us (83%)
  local copies, waits for them, and re-layouts  9.85 us (9%)
  matrix products  4.21 us (4%)
  other arithmetic  3.63 us (3%)
    pallas_call x3, Pallas kernels, with_halo(): pl.pallas_call(functools.partial(halo_kernel, before, after), in_specs=[p...  28.3 us
    pallas_call x3, Pallas kernels, level(): pl.pallas_call(functools.partial(level_kernel, stride, factor, bias_at),...  27 us
    pallas_call x1, Pallas kernels, encode_all(): pl.pallas_call(encode_kernel, in_specs=[vmem] * 7, out_specs=[vmem, vmem]...  22.7 us
    pallas_call x1, Pallas kernels, scatter_max(): pl.pallas_call(scatter_kernel, in_specs=[pl.BlockSpec(memory_space=pltpu....  10 us
    unnamed x16, local copies, waits for them, and re-layouts  4.31 us
    dot_general x3, matrix products, lift_layer(): jnp.einsum('oak,ijk->oiaj', weight, wide, preferred_element_type=jnp.floa...  4.21 us
    concatenate x1, local copies, waits for them, and re-layouts, on_device(): return jnp.concatenate([near, middle, distant], axis=0)  3.44 us

profile of v4, /device:TPU:9, one launch (start us, length us, event | category | flops | bytes accessed | tf_op | source)
XLA Modules:
  0.0 107.6 jit_solution(15538476435254395707)
XLA Ops:
  0.0 0.0 copy-start
  0.0 1.3 %reshape.76.bias_ref = f32[1,1408]{1,0:T(1,128)} reshape(f32[1408]{0:T(1024)} %param.31) | data formatting | bytes 11264 | tf_op jit(solution)/shard_map/reshape | solution.py:498
  1.3 1.4 %copy.21.embed_ref = bf16[64,9]{1,0:T(8,128)(2,1)} copy(bf16[64,9]{0,1:T(8,128)(2,1)} %param.20) | data formatting | bytes 2304 | tf_op args[4]
  2.7 1.8 %prepare.1 = (bf16[4,256,144]{2,1,0:T(8,128)(2,1)}, bf16[256,256]{1,0:T(8,128)(2,1)}, f32[256,1]{1,0:T(8,128)}, f32[64,1]{1,0:T(8,128)}) custom-call(bf16[64,9]{1,0:T(8,128)(2,1)} %copy.21.embed_ref, bf16[64,64]{1,0:T(8,128)(2,1)} %mix_ref.1, f32[1,1408]{1,0:T(1,128)} %reshape.76.bias_ref), custom_call_target="tpu_custom_call" | custom-call | tf_op jit(solution)/shard_map/prepare/pallas_call | solution.py:136
  4.4 1.3 %fusion.13 = s32[4096]{0:T(1024)} fusion(s32[4096]{0:T(1024)} %param.17), kind=kLoop, calls=%fused_computation.27 | loop fusion | flops 147456 | bytes 32768 | tf_op jit(solution)/shard_map/add | solution.py:497
  5.8 1.4 %compare_select_fusion.count_ref = s32[16,1,256]{2,1,0:T(1,128)} fusion(s32[16,1,256]{2,1,0:T(1,128)} %bitcast.63, s32[16]{0:T(128)} %param.19), kind=kLoop, calls=%fused_computation.14 | loop fusion | flops 8192 | bytes 32832 | tf_op jit(solution)/shard_map/jit(_where)/select_n | solution.py:495
  7.2 22.7 %encode_send.1 = (bf16[16,64,256]{2,1,0:T(8,128)(2,1)}, s32[16,1,256]{2,1,0:T(1,128)}) custom-call(bf16[9,32,4096]{2,1,0:T(8,128)(2,1)} %x_ref.1, s32[16,1,256]{2,1,0:T(1,128)} %compare_select_fusion.count_ref, s32[16,1,256]{2,1,0:T(1,128)} %bitcast.61, bf16[4,256,144]{2,1,0:T(8,128)(2,1)} %get-tuple-element.15.w1_ref, ...), custom_call_target="tpu_custom_call" | custom-call | tf_op jit(solution)/shard_map/encode_send/pallas_call | solution.py:148
  29.9 10.0 %scatter_max.1 = bf16[4096,64]{1,0:T(8,128)(2,1)} custom-call(s32[4096]{0:T(1024)} %bitcast.62, bf16[16,64,256]{2,1,0:T(8,128)(2,1)} %get-tuple-element.20.vec_ref), custom_call_target="tpu_custom_call" | custom-call | tf_op jit(solution)/shard_map/scatter_max/pallas_call | solution.py:201
  39.9 8.7 %halo_0.1.ext_ref = bf16[20,288,64]{2,1,0:T(8,128)(2,1)} custom-call(bf16[16,256,64]{2,1,0:T(8,128)(2,1)} %bitcast.58), custom_call_target="tpu_custom_call" | custom-call | tf_op jit(solution)/shard_map/halo_0/pallas_call | solution.py:323
  48.6 0.0 copy-start.4
  48.6 13.0 %level_0.1 = (bf16[16,256,64]{2,1,0:T(8,128)(2,1)}, bf16[1,16,128]{2,1,0:T(8,128)(2,1)}) custom-call(bf16[20,288,64]{2,1,0:T(8,128)(2,1)} %halo_0.1.ext_ref, bf16[3,3,64,64]{3,2,1,0:T(8,128)(2,1)} %wa_ref.3, bf16[3,3,64,64]{3,2,1,0:T(8,128)(2,1)} %wb_ref.3, f32[1,1408]{1,0:T(1,128)} %reshape.76.bias_ref), custom_call_target="tpu_custom_call" | custom-call | tf_op jit(solution)/shard_map/level_0/pallas_call | solution.py:425
  61.6 10.3 %halo_1.1.ext_ref = bf16[21,288,64]{2,1,0:T(8,128)(2,1)} custom-call(bf16[16,256,64]{2,1,0:T(8,128)(2,1)} %get-tuple-element.21.x_ref), custom_call_target="tpu_custom_call" | custom-call | tf_op jit(solution)/shard_map/halo_1/pallas_call | solution.py:323
  71.9 0.0 copy-done.4
  71.9 0.9 copy.23.wa_ref
  72.8 0.0 copy-start.3
  72.8 7.3 %level_1.1 = (bf16[8,128,128]{2,1,0:T(8,128)(2,1)}, bf16[8,256,256]{2,1,0:T(8,128)(2,1)}) custom-call(bf16[21,288,64]{2,1,0:T(8,128)(2,1)} %halo_1.1.ext_ref, bf16[3,3,128,64]{3,2,1,0:T(8,128)(2,1)} %copy.23.wa_ref, bf16[3,3,128,128]{3,2,1,0:T(8,128)(2,1)} %wb_ref.4, f32[1,1408]{1,0:T(1,128)} %reshape.76.bias_ref), custom_call_target="tpu_custom_call" | custom-call | tf_op jit(solution)/shard_map/level_1/pallas_call | solution.py:425
  80.1 9.4 %halo_2.1.ext_ref = bf16[13,160,128]{2,1,0:T(8,128)(2,1)} custom-call(bf16[8,128,128]{2,1,0:T(8,128)(2,1)} %get-tuple-element.23.x_ref), custom_call_target="tpu_custom_call" | custom-call | tf_op jit(solution)/shard_map/halo_2/pallas_call | solution.py:323
  89.5 6.7 %level_2.1 = (bf16[4,64,256]{2,1,0:T(8,128)(2,1)}, bf16[4,256,1024]{2,1,0:T(8,128)(2,1)}) custom-call(bf16[13,160,128]{2,1,0:T(8,128)(2,1)} %halo_2.1.ext_ref, bf16[3,3,256,128]{3,2,1,0:T(8,128)(2,1)} %wa_ref.4, bf16[3,3,256,256]{3,2,1,0:T(8,128)(2,1)} %wb_ref.5, f32[1,1408]{1,0:T(1,128)} %reshape.76.bias_ref), custom_call_target="tpu_custom_call" | custom-call | tf_op jit(solution)/shard_map/level_2/pallas_call | solution.py:425
  96.2 0.0 copy-done.3
  96.2 1.3 %copy.26 = bf16[4,4,128,256]{2,3,1,0:T(8,128)(2,1)} copy(bf16[4,4,128,256]{3,2,1,0:T(8,128)(2,1)S(1)} %copy-done.3) | data formatting | bytes 2097152 | tf_op args[14]
  97.5 3.2 %fusion.2 = f32[4,256,128,4]{1,2,3,0:T(8,128)S(1)} fusion(bf16[128,4,1024,1]{0,2,1,3:T(8,128)(2,1)} %bitcast.59, bf16[4,256,1024]{2,1,0:T(8,128)(2,1)} %get-tuple-element.24), kind=kOutput, calls=%fused_computation.4 | convolution fusion | flops 1073741824 | bytes 5242880 | tf_op jit(solution)/shard_map/oak,ijk->oiaj/dot_general | solution.py:450
  100.7 0.0 copy-done.5
  100.8 0.1 copy.24
  100.9 0.0 copy-done.2
  100.9 0.5 fusion.8
  101.4 0.8 fusion.16
  102.2 0.6 fusion.1
  102.8 0.0 copy-done
  102.9 0.6 copy-done.1
  103.4 0.5 fusion.7
  103.9 0.3 pad_maximum_fusion
  104.2 3.4 %copy.28 = bf16[384,16,256]{2,1,0:T(8,128)(2,1)} copy(bf16[384,16,256]{2,0,1:T(8,128)(2,1)S(1)} %pad_maximum_fusion) | data formatting | bytes 6291456 | tf_op jit(solution)/shard_map/concatenate | solution.py:520
  (3 shorter events, 0.0 us)
Async XLA Ops:
  0.0 102.8 %copy-start = (bf16[1,1,128,64]{2,3,1,0:T(8,128)(2,1)S(1)}, bf16[1,1,128,64]{2,3,1,0:T(8,128)(2,1)}, u32[]{:S(2)}) copy-start(bf16[1,1,128,64]{2,3,1,0:T(8,128)(2,1)} %param.28) | copy-start | bytes 49156
  48.6 23.3 %copy-start.4 = (bf16[3,3,128,64]{2,3,1,0:T(8,128)(2,1)S(1)}, bf16[3,3,128,64]{2,3,1,0:T(8,128)(2,1)}, u32[]{:S(2)}) copy-start(bf16[3,3,128,64]{2,3,1,0:T(8,128)(2,1)} %param.24) | copy-start | bytes 442372
  72.8 23.4 %copy-start.3 = (bf16[4,4,128,256]{3,2,1,0:T(8,128)(2,1)S(1)}, bf16[4,4,128,256]{3,2,1,0:T(8,128)(2,1)}, u32[]{:S(2)}) copy-start(bf16[4,4,128,256]{3,2,1,0:T(8,128)(2,1)} %param.30) | copy-start | bytes 3145732
  97.5 3.3 %copy-start.5 = (bf16[2,2,128,128]{3,2,1,0:T(8,128)(2,1)S(1)}, bf16[2,2,128,128]{3,2,1,0:T(8,128)(2,1)}, u32[]{:S(2)}) copy-start(bf16[2,2,128,128]{3,2,1,0:T(8,128)(2,1)} %param.29) | copy-start | bytes 393220
  97.5 3.4 %copy-start.2 = (bf16[8,256,256]{2,1,0:T(8,128)(2,1)S(1)}, bf16[8,256,256]{2,1,0:T(8,128)(2,1)}, u32[]{:S(2)}) copy-start(bf16[8,256,256]{2,1,0:T(8,128)(2,1)} %get-tuple-element.22) | copy-start | bytes 3145732
  102.2 1.2 %copy-start.1 = (bf16[16,256,64]{2,1,0:T(8,128)(2,1)S(1)}, bf16[16,256,64]{2,1,0:T(8,128)(2,1)}, u32[]{:S(2)}) copy-start(bf16[16,256,64]{2,1,0:T(8,128)(2,1)} %get-tuple-element.21.x_ref) | copy-start | bytes 1572868
